TPU v7x, 32 devices: a whole 2x2x4 slice. The times are simulated.
32 devices in a mesh: dp: 8 (over y, x, core), tensor: 4 (over z).
Axes of the slice: x: 2, y: 2, z: 4, core: 2. Of those that a mesh axis runs over, the one named last changes fastest.
Arguments:
- hidden_in: bfloat16 [16384, 1024], P(('dp', 'tensor')), may hold values from -6 to 6
- cotangent: bfloat16 [16384, 1024], P(('dp', 'tensor')), may hold values from -6 to 6
- norm_gains: bfloat16 [1024, 2], P('dp'), may hold values from 0.5 to 1.5
- mixer_in: bfloat16 [1024, 1536], P('dp', 'tensor'), may hold values from -0.1875 to 0.1875
- branch_gate: bfloat16 [1024, 1536], P('dp', 'tensor'), may hold values from -0.1875 to 0.1875
- mixer_out: bfloat16 [1024, 1536], P('dp', 'tensor'), may hold values from -0.4375 to 0.4375
- input_gate: bfloat16 [128, 12, 128], P('dp', 'tensor'), may hold values from -0.5 to 0.5
- recur_gate: bfloat16 [128, 12, 128], P('dp', 'tensor'), may hold values from -0.5 to 0.5
- conv_kernel: bfloat16 [128, 4, 12], P('dp', None, 'tensor'), may hold values from -3 to 3
- conv_bias: bfloat16 [128, 12], P('dp', 'tensor'), may hold values from -4 to 4
- input_bias: bfloat16 [128, 12], P('dp', 'tensor'), may hold values from -6 to 6
- recur_bias: bfloat16 [128, 12], P('dp', 'tensor'), may hold values from -6 to 6
- decay_param: bfloat16 [128, 12], P('dp', 'tensor'), may hold values from 2 to 9
- mlp_gate: bfloat16 [1024, 3072], P('dp', 'tensor'), may hold values from -0.1875 to 0.1875
- mlp_up: bfloat16 [1024, 3072], P('dp', 'tensor'), may hold values from -0.1875 to 0.1875
- mlp_down: bfloat16 [1024, 3072], P('dp', 'tensor'), may hold values from -0.15625 to 0.15625
Outputs:
- hidden_out: bfloat16 [16384, 1024], P(('dp', 'tensor'))
- hidden_grad: float32 [16384, 1024], P(('dp', 'tensor'))
- norm_gains_grad: float32 [1024, 2], P(('dp', 'tensor'))
- mixer_in_grad: float32 [1024, 1536], P('dp', 'tensor')
- branch_gate_grad: float32 [1024, 1536], P('dp', 'tensor')
- mixer_out_grad: float32 [1024, 1536], P('dp', 'tensor')
- input_gate_grad: float32 [128, 12, 128], P('dp', 'tensor')
- recur_gate_grad: float32 [128, 12, 128], P('dp', 'tensor')
- conv_kernel_grad: float32 [128, 4, 12], P('dp', None, 'tensor')
- conv_bias_grad: float32 [128, 12], P('dp', 'tensor')
- input_bias_grad: float32 [128, 12], P('dp', 'tensor')
- recur_bias_grad: float32 [128, 12], P('dp', 'tensor')
- decay_param_grad: float32 [128, 12], P('dp', 'tensor')
- mlp_gate_grad: float32 [1024, 3072], P('dp', 'tensor')
- mlp_up_grad: float32 [1024, 3072], P('dp', 'tensor')
- mlp_down_grad: float32 [1024, 3072], P('dp', 'tensor')
All inputs are finite; a program needn't handle non-finite values.
Results may differ from a plain program's by a relative error of at most 0.02.
Values may be sent and summed in bfloat16 or wider, within the bound.
No kernel may reach another device: no remote copies, remote signals or barrier semaphores. Data moves between devices by JAX's collectives and lax.ppermute only.
A program may use at most 256 MiB of HBM per device.

v0:
```python
import jax
import jax.numpy as jnp
from jax import lax
from jax.experimental import pallas as pl
from jax.experimental.pallas import tpu as pltpu
from jax.sharding import PartitionSpec as P

BLOCK = 128
CONV = 4
HALO = 16
TILE = 64
GROUP = 256
ROWS = 32
epsilon = 1e-06
f32 = jnp.float32
bf16 = jnp.bfloat16
ROOT = 0.7978845608028654
CUBIC = 0.044715


def nn(left, right):
    return lax.dot_general(left, right, (((1,), (0,)), ((), ())), preferred_element_type=f32)


def nt(left, right):
    return lax.dot_general(left, right, (((1,), (1,)), ((), ())), preferred_element_type=f32)


def tn(left, right):
    return lax.dot_general(left, right, (((0,), (0,)), ((), ())), preferred_element_type=f32)


def gelu_parts(value):
    square = value * value
    curve = jnp.tanh(ROOT * value * (1.0 + CUBIC * square))
    half = 0.5 * (1.0 + curve)
    slope = half + (0.5 * ROOT) * value * (1.0 - curve * curve) * (1.0 + 3.0 * CUBIC * square)
    return value * half, slope


def one_minus_exp(value):
    series = 1.0 + value * (1.0 / 7.0)
    for term in (6.0, 5.0, 4.0, 3.0, 2.0):
        series = 1.0 + value * (1.0 / term) * series
    return jnp.where(value > -0.25, -value * series, 1.0 - jnp.exp(value))


def scan_rows(decay_ref, drive_ref, offset, out_ref, out_offset, total_ref, length, reverse):
    width = drive_ref.shape[1]
    rows = lax.broadcasted_iota(jnp.int32, (8, width), 0)
    steps = length // 8

    def body(step, carry):
        state, product = carry
        at = (steps - 1 - step) if reverse else step
        start = pl.multiple_of(at * 8, 8)
        decay = decay_ref[pl.ds(start, 8 + 8 * (offset > 0)), :][offset : offset + 8]
        drive = drive_ref[pl.ds(start, 8), :]
        for shift in (1, 2, 4):
            if reverse:
                inside = rows < 8 - shift
                amount = 8 - shift
            else:
                inside = rows >= shift
                amount = shift
            drive = drive + decay * jnp.where(inside, pltpu.roll(drive, amount, 0), 0.0)
            decay = decay * jnp.where(inside, pltpu.roll(decay, amount, 0), 1.0)
        state = drive + decay * state
        product = decay * product
        out_ref[pl.ds(start + out_offset, 8), :] = state
        total_ref[pl.ds(start, 8), :] = product
        edge = 0 if reverse else 7
        return (
            jnp.broadcast_to(state[edge : edge + 1], (8, width)),
            jnp.broadcast_to(product[edge : edge + 1], (8, width)),
        )

    lax.fori_loop(0, steps, body, (jnp.zeros((8, width), f32), jnp.ones((8, width), f32)))


def tiles(length, body):
    def step(index, carry):
        body(pl.multiple_of(index * TILE, TILE))
        return carry

    lax.fori_loop(0, length // TILE, step, 0)


def mix_in_kernel(
    normed_ref, low_ref, high_ref, rgate_ref, igate_ref, table_ref,
    branch_ref, conv_ref, open_ref, flow_ref, local_ref, product_ref,
    conv_low, rec_buf, inp_buf, decay_buf,
):
    length = conv_ref.shape[0]
    half = low_ref.shape[0]
    branch_ref[...] = nn(normed_ref[:, :half], low_ref[...]) + nn(normed_ref[:, half:], high_ref[...])
    for part in range(GROUP // BLOCK):
        lanes = slice(part * BLOCK, (part + 1) * BLOCK)

        def convolve(start):
            window = branch_ref[pl.ds(start + HALO - 8, TILE + 8), lanes]
            result = table_ref[4:5, lanes] + table_ref[0:1, lanes] * window[8:]
            for offset in range(1, CONV):
                result = result + table_ref[offset : offset + 1, lanes] * window[8 - offset : 8 - offset + TILE]
            conv_ref[pl.ds(start, TILE), lanes] = result
            conv_low[pl.ds(start, TILE), lanes] = result.astype(bf16)

        tiles(length, convolve)
        rec_buf[:, lanes] = nn(conv_low[:, lanes], rgate_ref[part])
        inp_buf[:, lanes] = nn(conv_low[:, lanes], igate_ref[part])

        def gates(start):
            rows = pl.ds(start, TILE)
            recur_open = jax.nn.sigmoid(rec_buf[rows, lanes] + table_ref[6:7, lanes])
            inflow = jax.nn.sigmoid(inp_buf[rows, lanes] + table_ref[5:6, lanes])
            log_decay = recur_open * table_ref[7:8, lanes]
            multiplier = jnp.sqrt(one_minus_exp(2.0 * log_decay))
            open_ref[rows, lanes] = recur_open
            flow_ref[rows, lanes] = inflow
            decay_buf[rows, lanes] = jnp.exp(log_decay)
            rec_buf[rows, lanes] = multiplier * inflow * conv_ref[rows, lanes]

        tiles(length, gates)
    scan_rows(decay_buf, rec_buf, 0, local_ref, 0, product_ref, length, False)


def mix_out_kernel(
    normed_ref, low_ref, high_ref, local_ref, product_ref, enter_ref, sum_ref,
    pre_ref, states_ref, mixed_ref, total_ref,
):
    length = local_ref.shape[0]
    half = low_ref.shape[0]

    @pl.when(pl.program_id(0) == 0)
    def _():
        total_ref[...] = sum_ref[...].astype(f32)

    pre_ref[...] = nn(normed_ref[HALO:, :half], low_ref[:, :GROUP]) + nn(normed_ref[HALO:, half:], high_ref[:, :GROUP])
    states_ref[0:8, :] = jnp.broadcast_to(enter_ref[0:1, :], (8, GROUP))
    for part in range(GROUP // BLOCK):
        lanes = slice(part * BLOCK, (part + 1) * BLOCK)

        def mix(start):
            rows = pl.ds(start, TILE)
            states = local_ref[rows, lanes] + product_ref[rows, lanes] * enter_ref[0:1, lanes]
            states_ref[pl.ds(start + 8, TILE), lanes] = states
            gate = pre_ref[rows, lanes]
            curve = jnp.tanh(ROOT * gate * (1.0 + CUBIC * gate * gate))
            mixed_ref[rows, lanes] = (states * (gate * (0.5 * (1.0 + curve)))).astype(bf16)

        tiles(length, mix)
    total_ref[:, :half] += nt(mixed_ref[...], low_ref[:, GROUP:])
    total_ref[:, half:] += nt(mixed_ref[...], high_ref[:, GROUP:])


def mlp_kernel(
    chunks_ref, normed_ref, normed_t_ref, cot_ref, cot_t_ref, gate_ref, up_ref, down_ref, sum_ref, back_ref,
    total_ref, grad_ref, low_grad_ref, high_grad_ref,
    pre, hidden, pre_low, act,
):
    length, model = normed_ref.shape
    half = model // 2
    first = sum_ref is None

    @pl.when(pl.program_id(0) == 0)
    def _():
        if first:
            total_ref[...] = jnp.zeros_like(total_ref)
            grad_ref[...] = jnp.zeros_like(grad_ref)
        else:
            total_ref[...] = sum_ref[...]
            grad_ref[...] = back_ref[...]

    gate = gate_ref[...].reshape(model, GROUP)
    up_weights = up_ref[...].reshape(model, GROUP)
    down = down_ref[...].reshape(model, GROUP)
    pre[:, :GROUP] = nn(normed_ref[...], gate)
    pre[:, GROUP:] = nn(normed_ref[...], up_weights)
    act[...] = nn(cot_ref[...], down)
    for part in range(GROUP // BLOCK):
        lanes = slice(part * BLOCK, (part + 1) * BLOCK)
        up_lanes = slice(GROUP + part * BLOCK, GROUP + (part + 1) * BLOCK)

        def activate(start):
            rows = pl.ds(start, TILE)
            value, slope = gelu_parts(pre[rows, lanes])
            up = pre[rows, up_lanes]
            grad = act[rows, lanes]
            hidden[rows, lanes] = (value * up).astype(bf16)
            pre_low[rows, lanes] = (grad * up * slope).astype(bf16)
            pre_low[rows, up_lanes] = (grad * value).astype(bf16)

        tiles(length, activate)
    total_ref[...] += nt(hidden[...], down)
    grad_ref[...] += nt(pre_low[:, :GROUP], gate) + nt(pre_low[:, GROUP:], up_weights)
    low_grad_ref[:, : 2 * GROUP] = nn(normed_t_ref[:half], pre_low[...]).astype(bf16)
    high_grad_ref[:, : 2 * GROUP] = nn(normed_t_ref[half:], pre_low[...]).astype(bf16)
    low_grad_ref[:, 2 * GROUP :] = nn(cot_t_ref[:half], hidden[...]).astype(bf16)
    high_grad_ref[:, 2 * GROUP :] = nn(cot_t_ref[half:], hidden[...]).astype(bf16)


def lane_block(index):
    return pl.ds(pl.multiple_of(index * BLOCK, BLOCK), BLOCK)


def order_kernel(places_ref, hidden_ref, cot_ref, hidden_out_ref, cot_out_ref, cot_t_ref):
    for place in range(hidden_ref.shape[1] // BLOCK):
        lanes = slice(place * BLOCK, (place + 1) * BLOCK)
        hidden_out_ref[:, lanes] = hidden_ref[:, lane_block(places_ref[place])]
        cot_out_ref[:, lanes] = cot_ref[:, lane_block(places_ref[place])]
    cot_t_ref[...] = cot_out_ref[...].T


def row_loop(length, rows, body, start):
    def step(index, carry):
        return body(pl.ds(pl.multiple_of(index * rows, rows), rows), carry)

    return lax.fori_loop(0, length // rows, step, start)


def scale_of(values):
    return lax.rsqrt(jnp.mean(values * values, axis=1, keepdims=True) + epsilon)


def norm_kernel(places_ref, hidden_ref, first_ref, gains_ref, normed_ref, normed_t_ref, first_buf):
    length = hidden_ref.shape[0]
    for place in range(hidden_ref.shape[1] // BLOCK):
        lanes = slice(place * BLOCK, (place + 1) * BLOCK)
        first_buf[:, lanes] = first_ref[:, lane_block(places_ref[place])].astype(f32)
    first = first_buf[...]
    normed_ref[:HALO, :] = (first * scale_of(first) * gains_ref[0:1, :]).astype(bf16)

    def body(rows, carry):
        values = hidden_ref[rows, :].astype(f32)
        normed_ref[pl.ds(rows.start + HALO, rows.size), :] = (values * scale_of(values) * gains_ref[0:1, :]).astype(bf16)
        return carry

    row_loop(length, ROWS, body, 0)
    normed_t_ref[...] = normed_ref[HALO:, :].T


def second_norm_kernel(places_ref, middle_ref, gains_ref, normed_ref, normed_t_ref, buffer):
    length, model = middle_ref.shape

    def body(rows, carry):
        values = middle_ref[rows, :]
        buffer[rows, :] = (values * scale_of(values) * gains_ref[1:2, :]).astype(bf16)
        return carry

    row_loop(length, ROWS, body, 0)
    normed_t_ref[...] = buffer[...].T
    for place in range(model // BLOCK):
        normed_ref[:, lane_block(places_ref[place])] = buffer[:, place * BLOCK : (place + 1) * BLOCK]


def norm_back(values, grad, gain):
    scale = scale_of(values)
    unit = values * scale
    scaled = grad * gain
    return scale * (scaled - unit * jnp.mean(scaled * unit, axis=1, keepdims=True)), grad * unit


def fold_rows(value):
    rows, width = value.shape
    return jnp.sum(value.reshape(rows // 8, 8, width), axis=0)


def middle_kernel(
    places_ref, middle_ref, total_ref, grad_ref, cot_ref, gains_ref,
    out_ref, middle_grad_ref, low_ref, low_t_ref, gain_ref, buffer, own_total, own_grad,
):
    length, model = middle_ref.shape
    for place in range(model // BLOCK):
        lanes = slice(place * BLOCK, (place + 1) * BLOCK)
        own_total[:, lanes] = total_ref[:, lane_block(places_ref[place])]
        own_grad[:, lanes] = grad_ref[:, lane_block(places_ref[place])]

    def body(rows, carry):
        middle = middle_ref[rows, :]
        change, part = norm_back(middle, own_grad[rows, :], gains_ref[1:2, :])
        middle_grad = cot_ref[rows, :].astype(f32) + change
        middle_grad_ref[rows, :] = middle_grad
        low_ref[rows, :] = middle_grad.astype(bf16)
        buffer[rows, :] = (middle + own_total[rows, :]).astype(bf16)
        return carry + fold_rows(part)

    total = row_loop(length, ROWS, body, jnp.zeros((8, model), f32))
    gain_ref[...] = jnp.sum(total, axis=0, keepdims=True)
    low_t_ref[...] = low_ref[...].T
    for place in range(model // BLOCK):
        out_ref[:, lane_block(places_ref[place])] = buffer[:, place * BLOCK : (place + 1) * BLOCK]


def final_kernel(places_ref, hidden_ref, grad_ref, middle_grad_ref, gains_ref, out_ref, gain_ref, buffer):
    length, model = hidden_ref.shape

    def body(rows, carry):
        change, part = norm_back(hidden_ref[rows, :].astype(f32), grad_ref[rows, :], gains_ref[0:1, :])
        buffer[rows, :] = middle_grad_ref[rows, :] + change
        return carry + fold_rows(part)

    total = row_loop(length, ROWS, body, jnp.zeros((8, model), f32))
    gain_ref[...] = jnp.sum(total, axis=0, keepdims=True)
    for place in range(model // BLOCK):
        out_ref[:, lane_block(places_ref[place])] = buffer[:, place * BLOCK : (place + 1) * BLOCK]


def tables_kernel(places_ref, *refs, sub, local_blocks, chunks):
    sources, (rgate_ref, igate_ref, table_ref, gains_ref) = refs[:-4], refs[-4:]
    rows_each = 2 * local_blocks * sub
    kinds = 2 * CONV
    count = places_ref.shape[0]
    size = sources[0].shape[0] * 2 // count
    sums = [jnp.zeros((kinds * local_blocks, BLOCK), f32)] * chunks
    for place in range(count):
        side = place // (count // 2)
        top = (place % (count // 2)) * size
        natural = places_ref[place]
        for at in range(chunks):
            source = sources[at // 2 * 2 + side]
            lanes = slice(at % 2 * BLOCK, (at % 2 + 1) * BLOCK)
            for which, gate_ref in enumerate((rgate_ref, igate_ref)):
                for block in range(local_blocks):
                    start = top + (which * local_blocks + block) * sub
                    gate_ref[at * local_blocks + block, pl.ds(pl.multiple_of(natural * sub, sub), sub), :] = source[start : start + sub, lanes]
            sums[at] = sums[at] + source[top + rows_each : top + rows_each + kinds * local_blocks, lanes].astype(f32)
        start = top + rows_each + kinds * local_blocks
        gains_ref[:, place * BLOCK : (place + 1) * BLOCK] = sources[side][start : start + 2, :BLOCK].astype(f32)
    for at in range(chunks):
        for block in range(local_blocks):
            column = (at * local_blocks + block) * BLOCK
            for kind in range(kinds):
                row = kind * local_blocks + block
                table_ref[kind : kind + 1, column : column + BLOCK] = sums[at][row : row + 1]


def small_grads_kernel(places_ref, rgrad_ref, igrad_ref, sums_ref, *targets, sub, local_blocks, chunks):
    kinds = 2 * CONV
    rows_each = 2 * local_blocks * sub
    count = places_ref.shape[0]
    size = targets[0].shape[0] * 2 // count
    spare = size - rows_each - kinds * local_blocks
    vectors = []
    for at in range(chunks):
        rows = []
        for kind in range(kinds):
            for block in range(local_blocks):
                column = (at * local_blocks + block) * BLOCK
                rows.append(sums_ref[kind : kind + 1, column : column + BLOCK])
        vectors.append(jnp.concatenate(rows, axis=0))
    for place in range(count):
        side = place // (count // 2)
        top = (place % (count // 2)) * size
        natural = places_ref[place]
        for at in range(chunks):
            target = targets[at // 2 * 2 + side]
            lanes = slice(at % 2 * BLOCK, (at % 2 + 1) * BLOCK)
            for which, grad_ref in enumerate((rgrad_ref, igrad_ref)):
                for block in range(local_blocks):
                    start = top + (which * local_blocks + block) * sub
                    target[start : start + sub, lanes] = grad_ref[
                        at * local_blocks + block, pl.ds(pl.multiple_of(natural * sub, sub), sub), :
                    ].astype(bf16)
            rest = jnp.concatenate([vectors[at], jnp.zeros((spare, BLOCK), f32)], axis=0)
            target[top + rows_each : top + size, lanes] = rest.astype(bf16)


def mix_back_kernel(
    grad_low_ref, grad_t_ref, normed_t_ref, low_ref, high_ref, pre_ref, states_ref, mixed_ref, open_ref, table_ref, sum_ref,
    total_ref, local_ref, product_ref, edge_ref, low_grad_ref, high_grad_ref,
    mixed_grad, drive, pre_low, decay_buf, *, first,
):
    length = pre_ref.shape[0]
    half = low_ref.shape[0]

    @pl.when(pl.program_id(0) == 0)
    def _():
        total_ref[...] = jnp.zeros_like(total_ref) if first else sum_ref[...]

    mixed_grad[...] = nn(grad_low_ref[:, :half], low_ref[:, GROUP:]) + nn(grad_low_ref[:, half:], high_ref[:, GROUP:])
    decay_buf[pl.ds(length, 8), :] = jnp.ones((8, GROUP), f32)
    for part in range(GROUP // BLOCK):
        lanes = slice(part * BLOCK, (part + 1) * BLOCK)

        def back(start):
            rows = pl.ds(start, TILE)
            value, slope = gelu_parts(pre_ref[rows, lanes])
            grad = mixed_grad[rows, lanes]
            pre_low[rows, lanes] = (grad * states_ref[pl.ds(start + 8, TILE), lanes] * slope).astype(bf16)
            drive[rows, lanes] = grad * value
            decay_buf[rows, lanes] = jnp.exp(open_ref[rows, lanes] * table_ref[7:8, lanes])

        tiles(length, back)
    scan_rows(decay_buf, drive, 1, local_ref, 0, product_ref, length, True)
    edge_ref[0:1, :] = decay_buf[0:1, :] * local_ref[0:1, :]
    edge_ref[1:2, :] = decay_buf[0:1, :] * product_ref[0:1, :]
    total_ref[:, :half] += nt(pre_low[...], low_ref[:, :GROUP])
    total_ref[:, half:] += nt(pre_low[...], high_ref[:, :GROUP])
    low_grad_ref[:, :GROUP] = nn(normed_t_ref[:half], pre_low[...]).astype(bf16)
    high_grad_ref[:, :GROUP] = nn(normed_t_ref[half:], pre_low[...]).astype(bf16)
    low_grad_ref[:, GROUP:] = nn(grad_t_ref[:half], mixed_ref[...]).astype(bf16)
    high_grad_ref[:, GROUP:] = nn(grad_t_ref[half:], mixed_ref[...]).astype(bf16)


def gate_back_kernel(
    local_ref, product_ref, enter_ref, states_ref, open_ref, flow_ref, conv_ref, branch_ref, rgate_ref, igate_ref, table_ref,
    conv_grad_ref, rgrad_ref, igrad_ref, sums_ref,
    rec_low, inp_low, conv_low,
):
    length = local_ref.shape[0]
    for part in range(GROUP // BLOCK):
        lanes = slice(part * BLOCK, (part + 1) * BLOCK)

        def back(index, sums):
            start = pl.multiple_of(index * TILE, TILE)
            rows = pl.ds(start, TILE)
            carried = local_ref[rows, lanes] + product_ref[rows, lanes] * enter_ref[0:1, lanes]
            recur_open = open_ref[rows, lanes]
            inflow = flow_ref[rows, lanes]
            conv_out = conv_ref[rows, lanes]
            rate = table_ref[7:8, lanes]
            log_decay = recur_open * rate
            decay = jnp.exp(log_decay)
            multiplier = jnp.sqrt(one_minus_exp(2.0 * log_decay))
            before = states_ref[pl.ds(start, TILE + 8), lanes][7 : 7 + TILE]
            weighted = carried * inflow
            decay_grad = carried * before * decay - weighted * conv_out * decay * decay / multiplier
            scaled = decay_grad * recur_open
            rec_grad = rate * scaled * (1.0 - recur_open)
            direct = weighted * multiplier
            inp_grad = direct * conv_out * (1.0 - inflow)
            rec_low[rows, lanes] = rec_grad.astype(bf16)
            inp_low[rows, lanes] = inp_grad.astype(bf16)
            conv_low[rows, lanes] = conv_out.astype(bf16)
            conv_grad_ref[rows, lanes] = direct

            def fold(value):
                return jnp.sum(value.reshape(TILE // 8, 8, BLOCK), axis=0)

            return (sums[0] + fold(rec_grad), sums[1] + fold(inp_grad), sums[2] + fold(scaled))

        zero = jnp.zeros((8, BLOCK), f32)
        sums = lax.fori_loop(0, length // TILE, back, (zero, zero, zero))
        for row, value in zip((2, 1, 3), sums):
            sums_ref[row : row + 1, lanes] = jnp.sum(value, axis=0, keepdims=True)
        rgrad_ref[part] = tn(conv_low[:, lanes], rec_low[:, lanes])
        igrad_ref[part] = tn(conv_low[:, lanes], inp_low[:, lanes])
        conv_grad_ref[:, lanes] += nt(rec_low[:, lanes], rgate_ref[part]) + nt(inp_low[:, lanes], igate_ref[part])

        def taps(index, sums):
            start = pl.multiple_of(index * TILE, TILE)
            grad = conv_grad_ref[pl.ds(start, TILE), lanes]

            def fold(value):
                return jnp.sum(value.reshape(TILE // 8, 8, BLOCK), axis=0)

            window = branch_ref[pl.ds(start + HALO - 8, TILE + 8), lanes]
            new = [sums[0] + fold(grad)]
            for offset in range(CONV):
                new.append(sums[offset + 1] + fold(grad * window[8 - offset : 8 - offset + TILE]))
            return tuple(new)

        sums = lax.fori_loop(0, length // TILE, taps, (zero,) * (CONV + 1))
        for row, value in zip((0, 4, 5, 6, 7), sums):
            sums_ref[row : row + 1, lanes] = jnp.sum(value, axis=0, keepdims=True)


def branch_back_kernel(
    conv_grad_ref, after_ref, table_ref, normed_t_ref, low_ref, high_ref, sum_ref, small_refs,
    total_ref, low_grad_ref, high_grad_ref,
    padded, branch_low, *, groups,
):
    length = conv_grad_ref.shape[0]
    half = low_ref.shape[0]

    @pl.when(pl.program_id(0) == 0)
    def _():
        total_ref[...] = sum_ref[...]

    @pl.when(pl.program_id(0) < groups)
    def _():
        padded[pl.ds(0, length), :] = conv_grad_ref[...]
        padded[pl.ds(length, 8), :] = after_ref[...]
        for part in range(GROUP // BLOCK):
            lanes = slice(part * BLOCK, (part + 1) * BLOCK)

            def back(start):
                window = padded[pl.ds(start, TILE + 8), lanes]
                result = table_ref[0:1, lanes] * window[:TILE]
                for offset in range(1, CONV):
                    result = result + table_ref[offset : offset + 1, lanes] * window[offset : offset + TILE]
                branch_low[pl.ds(start, TILE), lanes] = result.astype(bf16)

            tiles(length, back)
        total_ref[:, :half] += nt(branch_low[...], low_ref[...])
        total_ref[:, half:] += nt(branch_low[...], high_ref[...])
        low_grad_ref[...] = nn(normed_t_ref[:half], branch_low[...]).astype(bf16)
        high_grad_ref[...] = nn(normed_t_ref[half:], branch_low[...]).astype(bf16)

    if small_refs:

        @pl.when(pl.program_id(0) == groups)
        def _():
            low_grad_ref[...] = small_refs[0][...]
            high_grad_ref[...] = small_refs[1][...]


def join_kernel(*refs, columns):
    parts, outs = refs[: -len(columns)], refs[-len(columns) :]
    for out_ref, places in zip(outs, columns):
        to = 0
        for start, size in places:
            total = parts[0][:, start : start + size].astype(f32)
            for part in parts[1:]:
                total = total + part[:, start : start + size].astype(f32)
            out_ref[:, to : to + size] = total
            to += size


def fixed(shape):
    return pl.BlockSpec(shape, lambda g: (0,) * len(shape))


def lanes_until(rows, last):
    return pl.BlockSpec((rows, GROUP), lambda g: (0, jnp.minimum(g, last)))


def lanes_of(rows, width=GROUP):
    return pl.BlockSpec((rows, width), lambda g: (0, g))


def blocks_of():
    return pl.BlockSpec((GROUP // BLOCK, BLOCK, BLOCK), lambda g: (g, 0, 0))


def shaped(*dims, kind=f32):
    return jax.ShapeDtypeStruct(dims, kind)


VMEM_LIMIT = 28 * 1024 * 1024
PARAMS = pltpu.CompilerParams(dimension_semantics=("arbitrary",), vmem_limit_bytes=VMEM_LIMIT)


ANYWHERE = pl.BlockSpec(memory_space=pl.ANY)
SCALARS = pl.BlockSpec(memory_space=pltpu.SMEM)


SPANS = {
    "order_kernel": 4, "tables_of": 2, "norm_kernel": 6, "mix_in_kernel": 14, "mix_out_kernel": 10,
    "second_norm_kernel": 6, "mlp_kernel": 17, "middle_kernel": 12, "mix_back": 18, "gate_back_kernel": 11,
    "branch_back": 8, "final_kernel": 10, "small_grads": 3, "join": 2,
}


def call(kernel, steps, in_specs, out_specs, out_shape, scratch, hold=()):
    count = len(in_specs)
    name = getattr(kernel, "func", kernel).__name__

    def body(*refs):
        kernel(*refs[:count], *refs[count + len(hold) :])

    run = pl.pallas_call(
        body,
        grid=(steps,),
        in_specs=list(in_specs) + [ANYWHERE] * len(hold),
        out_specs=out_specs,
        out_shape=out_shape,
        scratch_shapes=scratch,
        compiler_params=PARAMS,
        name=name,
        cost_estimate=pl.CostEstimate(flops=SPANS[name] * 1150 * 10**6, bytes_accessed=0, transcendentals=0),
    )
    return lambda *args: run(*args, *hold)


def make_per_device(dp_size, tensor_size):
    pairs = tensor_size // 2
    dp_bits = [1 << bit for bit in range(dp_size.bit_length() - 1)]
    order_one = dp_bits[1:] + dp_bits[:1]
    order_two = dp_bits[2:3] + dp_bits[1:2] + dp_bits[3:] + dp_bits[:1]
    orders = (order_one, order_two)
    position_of = {bit: place for place, bit in enumerate(order_one)}

    def swap_dp(values, bit):
        return lax.ppermute(values, "dp", [(at, at ^ bit) for at in range(dp_size)])

    def swap_tensor(values, bit):
        return lax.ppermute(values, "tensor", [(at, at ^ bit) for at in range(tensor_size)])

    def relative(pieces, index):
        bit = 1
        while bit < len(pieces):
            flag = (index & bit) != 0
            pieces = [jnp.where(flag, pieces[at ^ bit], piece) for at, piece in enumerate(pieces)]
            bit *= 2
        return pieces

    place_index = [
        sum(bit for bit in dp_bits if place & (1 << position_of[bit])) for place in range(dp_size)
    ]

    def split_lanes(values, count):
        width = values.shape[1] // count
        return [values[:, at * width : (at + 1) * width] for at in range(count)]

    class Gather:
        def __init__(self, values, order):
            self.rows, self.left, self.done = values.shape[0], list(order), []
            self.send(values)

        def send(self, values):
            self.values, self.bit = values, self.left.pop(0)
            self.received = swap_dp(values, self.bit)

        def take(self, received):
            if not self.left:
                self.received, self.last = None, received
                return
            values, rows = self.values, self.rows
            if all(position_of[other] < position_of[self.bit] for other in self.done):
                values = jnp.concatenate([values, received], axis=0)
            else:
                pieces = []
                for at in range(0, values.shape[0], rows):
                    pieces += [values[at : at + rows], received[at : at + rows]]
                values = jnp.concatenate(pieces, axis=0)
            self.done.append(self.bit)
            self.send(values)

        def finish(self):
            while self.received is not None:
                self.take(self.received)
            return self.values, self.last

    def round_of(travellers, *others):
        travellers = [one for one in travellers if one.received is not None]
        found = lax.optimization_barrier(tuple(one.received for one in travellers) + others)
        for one, received in zip(travellers, found):
            one.take(received)
        return list(found[len(travellers) :])

    def add(one, two):
        return (one.astype(f32) + two.astype(f32)).astype(one.dtype)

    class Scatter:
        def __init__(self, own, other, order, block_rows):
            self.left, self.block_rows = list(order[:-1]), block_rows
            self.values, self.received = own, swap_dp(other, order[-1])

        def halves(self, values, bit):
            rows = values.shape[0]
            if all(position_of[other] < position_of[bit] for other in self.left):
                return values[: rows // 2], values[rows // 2 :]
            starts = range(0, rows, self.block_rows)
            pieces = [values[at : at + self.block_rows] for at in starts]
            return jnp.concatenate(pieces[0::2], axis=0), jnp.concatenate(pieces[1::2], axis=0)

        def step(self, token=None):
            received = self.received
            if token is not None:
                received, token = lax.optimization_barrier((received, token))
            self.take(received)
            return token

        def take(self, received):
            if self.left:
                bit = self.left.pop()
                keep, send = self.halves(self.values, bit)
                keep_more, send_more = self.halves(received, bit)
                sent = add(send, send_more)
                self.values, self.received = add(keep, keep_more), swap_dp(sent, bit)
                self.mark = sent
            else:
                self.values, self.received = add(self.values, received), None
                self.mark = self.values

        def finish(self):
            while self.received is not None:
                self.step()
            return self.values

    def steps(scatters, token):
        for one in scatters:
            if one.received is not None:
                token = one.step(token)
        return token, [one.mark for one in scatters]

    def spread_tensor(values):
        return [values] + [swap_tensor(values, other) for other in range(1, tensor_size)]

    def join_parts(own, others, columns, hold):
        parts = [own] + [others[other] for other in range(1, tensor_size)]

        def join(*refs):
            join_kernel(*refs, columns=columns)

        rows = own.shape[0]
        widths = [sum(size for _, size in places) for places in columns]
        return call(
            join, 1, [fixed(own.shape)] * tensor_size, [fixed((rows, width)) for width in widths],
            [shaped(rows, width) for width in widths], [], hold=hold,
        )(*parts)

    def join_tensor(parts):
        total = parts[0].astype(f32)
        received = []
        for other in range(1, tensor_size):
            received.append(swap_tensor(parts[other], other))
            total = total + received[-1].astype(f32)
        return total, received

    def per_device(
        hidden_in, cotangent, norm_gains, mixer_in, branch_gate, mixer_out, input_gate, recur_gate,
        conv_kernel, conv_bias, input_bias, recur_bias, decay_param, mlp_gate, mlp_up, mlp_down,
    ):
        dp_at = lax.axis_index("dp")
        tensor_at = lax.axis_index("tensor")
        length, model = hidden_in.shape
        block_rows, chunk = mixer_in.shape
        half = model // 2
        hidden_chunk = mlp_gate.shape[1]
        sub = block_rows * BLOCK // model
        local_blocks = chunk // BLOCK
        pair_width = 2 * chunk
        groups = pair_width // GROUP
        mlp_groups = hidden_chunk // GROUP
        fast = block_rows == BLOCK and sub % 16 == 0
        natural_at = jnp.array(place_index, jnp.int32) ^ dp_at
        places = natural_at if fast else jnp.arange(model // BLOCK, dtype=jnp.int32)

        def features(values, back=False):
            if fast:
                return values
            pieces = jnp.stack(split_lanes(values, dp_size), axis=0)
            order = natural_at
            if back:
                order = jnp.zeros_like(natural_at).at[natural_at].set(jnp.arange(dp_size, dtype=jnp.int32))
            return jnp.concatenate(list(jnp.take(pieces, order, axis=0)), axis=1)

        first_rows = lax.ppermute(
            hidden_in[length - HALO :], "tensor", [(at, at + 1) for at in range(tensor_size - 1)]
        )

        def rows_first(table):
            return table.transpose(1, 0, 2).reshape(-1, BLOCK)

        vectors = jnp.concatenate(
            [conv_kernel.transpose(1, 2, 0).reshape(-1, sub)]
            + [table.T for table in (conv_bias, input_bias, recur_bias, decay_param)],
            axis=0,
        )
        owner = lax.broadcasted_iota(jnp.int32, (1, BLOCK), 1) // sub
        vectors = jnp.where(owner == dp_at, jnp.tile(vectors, (1, BLOCK // sub)), jnp.zeros((), bf16))
        gate_rows = 2 * local_blocks * sub
        vector_rows = vectors.shape[0]
        small_rows = (gate_rows + vector_rows + 2 + 15) // 16 * 16
        small = jnp.concatenate(
            [
                rows_first(recur_gate),
                rows_first(input_gate),
                vectors,
                jnp.pad(norm_gains.T, ((0, 0), (0, BLOCK - block_rows))),
                jnp.zeros((small_rows - gate_rows - vector_rows - 2, BLOCK), bf16),
            ],
            axis=0,
        )
        whole = fixed((length, model))
        turned = fixed((model, length))
        hidden_low, cot_low, cot_t = call(
            order_kernel, 1, [SCALARS, whole, whole], [whole, whole, turned],
            [shaped(length, model, kind=bf16), shaped(length, model, kind=bf16), shaped(model, length, kind=bf16)], [],
        )(places, features(hidden_in), features(cotangent))

        merged = fast and small_rows == block_rows

        def in_pairs_of(found):
            return [
                jnp.concatenate([one[:, :chunk], two[:, :chunk], one[:, chunk:], two[:, chunk:]], axis=1) if merged
                else jnp.concatenate([one, two], axis=1)
                for one, two in zip(found[0::2], found[1::2])
            ]

        def interleave(one, two):
            gate = jnp.concatenate([one[:, :chunk], two[:, :chunk]], axis=1)
            out = jnp.concatenate([one[:, chunk:], two[:, chunk:]], axis=1)
            pieces = []
            for at in range(groups):
                pieces += [gate[:, at * GROUP : (at + 1) * GROUP], out[:, at * GROUP : (at + 1) * GROUP]]
            return jnp.concatenate(pieces, axis=1)

        in_near = spread_tensor(jnp.concatenate([mixer_in, small], axis=1) if merged else mixer_in)
        *in_near[1:], first_rows, gate_weights, out_weights = lax.optimization_barrier(
            tuple(in_near[1:]) + (first_rows, branch_gate, mixer_out)
        )
        in_gathers = [Gather(values, orders[at % 2]) for at, values in enumerate(in_pairs_of(in_near))]
        out_near = spread_tensor(jnp.concatenate([gate_weights, out_weights], axis=1))
        *out_near[1:], hidden_low = round_of(in_gathers, *out_near[1:], hidden_low)
        out_gathers = [
            Gather(interleave(one, two), orders[at % 2]) for at, (one, two) in enumerate(zip(out_near[0::2], out_near[1::2]))
        ]
        round_of(in_gathers + out_gathers)
        in_pairs = [one.finish() for one in in_gathers]
        if not merged:
            small_low, small_high = Gather(jnp.concatenate(spread_tensor(small), axis=1), order_one).finish()
        mlp_weights = lax.all_gather(jnp.concatenate([mlp_gate, mlp_up, mlp_down], axis=1), ("dp", "tensor"), axis=0, tiled=False)
        mlp_weights = mlp_weights.reshape(dp_size, tensor_size, block_rows, 3 * hidden_chunk)

        kinds = 2 * CONV
        channels = tensor_size * chunk
        blocks = tensor_size * local_blocks
        if merged:
            small_spec = pl.BlockSpec((half, 2 * BLOCK), lambda g: (0, pair_width // (2 * BLOCK)))
            gate_spec = fixed((blocks, BLOCK, BLOCK))
            def tables_of(*args, **sizes):
                tables_kernel(*args, sub=sub, local_blocks=local_blocks, chunks=tensor_size)
            rgates, igates, table, gains = call(
                tables_of, 1, [SCALARS] + [small_spec] * tensor_size, [gate_spec, gate_spec, fixed((kinds, channels)), fixed((2, model))],
                [shaped(blocks, BLOCK, BLOCK, kind=bf16), shaped(blocks, BLOCK, BLOCK, kind=bf16), shaped(kinds, channels), shaped(2, model)], [],
            )(places, *[values for pair in in_pairs for values in pair])
        else:
            stacked = jnp.concatenate([small_low, small_high], axis=0).reshape(dp_size, small_rows, -1)
            order = jnp.zeros_like(natural_at).at[natural_at].set(jnp.arange(dp_size, dtype=jnp.int32))
            gates = jnp.take(stacked[:, :gate_rows], order, axis=0).reshape(dp_size, 2, local_blocks, sub, tensor_size, BLOCK)
            gates = gates.transpose(1, 4, 2, 0, 3, 5).reshape(2, blocks, BLOCK, BLOCK)
            rgates, igates = gates[0], gates[1]
            table = jnp.sum(stacked[:, gate_rows : gate_rows + vector_rows].astype(f32), axis=0)
            table = table.reshape(kinds, local_blocks, tensor_size, BLOCK).transpose(0, 2, 1, 3).reshape(kinds, channels)
            gains = stacked[:, gate_rows + vector_rows : gate_rows + vector_rows + 2, :block_rows]
            gains = gains.transpose(1, 0, 2).reshape(2, model).astype(f32)
        decay_rates = table[7:8]
        last_row = lax.broadcasted_iota(jnp.int32, table.shape, 0) == kinds - 1
        table = jnp.where(last_row, -8.0 * jax.nn.softplus(-table), table)

        full = length + HALO
        normed_one, normed_one_t = call(
            norm_kernel, 1, [SCALARS, whole, fixed((HALO, model)), fixed((2, model))], [fixed((full, model)), turned],
            [shaped(full, model, kind=bf16), shaped(model, length, kind=bf16)], [pltpu.VMEM((HALO, model), f32)],
        )(places, hidden_low, features(first_rows), gains)

        fed = []
        for pair in range(pairs):
            low, high = in_pairs[pair]
            part = slice(2 * pair * local_blocks, 2 * (pair + 1) * local_blocks)
            lanes = slice(pair * pair_width, (pair + 1) * pair_width)
            fed.append(
                call(
                    mix_in_kernel,
                    groups,
                    [fixed((full, model)), lanes_of(half), lanes_of(half), blocks_of(), blocks_of(), lanes_of(8)],
                    [lanes_of(full)] + [lanes_of(length)] * 5,
                    [shaped(full, pair_width)] + [shaped(length, pair_width)] * 5,
                    [pltpu.VMEM((length, GROUP), bf16)] + [pltpu.VMEM((length, GROUP), f32)] * 3,
                )(normed_one, low, high, rgates[part], igates[part], table[:, lanes])
            )
            fed[pair] = list(fed[pair])
        fed[-1][5:] = round_of(out_gathers, fed[-1][5])
        out_pairs = [one.finish() for one in out_gathers]

        def exchange(products, ends, later):
            mine = jnp.concatenate([products, ends], axis=0)
            found = [mine]
            for other in range(1, tensor_size):
                pieces = split_lanes(swap_tensor(mine, other), tensor_size)
                found.append(jnp.concatenate([pieces[at ^ other] for at in range(tensor_size)], axis=1))
            found = relative(found, tensor_at)
            state = jnp.zeros_like(ends)
            turn = range(tensor_size - 1, 0, -1) if later else range(tensor_size - 1)
            for at in turn:
                use = (at > tensor_at) if later else (at < tensor_at)
                state = jnp.where(use, found[at][0:1] * state + found[at][1:2], state)
            return state

        enter = exchange(
            jnp.concatenate([one[5][length - 1 :] for one in fed], axis=1),
            jnp.concatenate([one[4][length - 1 :] for one in fed], axis=1),
            False,
        )
        middle = hidden_low
        mixed = []
        for pair in range(pairs):
            low, high = out_pairs[pair]
            lanes = slice(pair * pair_width, (pair + 1) * pair_width)
            gate_pre, states, mixed_low, middle = call(
                mix_out_kernel,
                groups,
                [fixed((full, model)), lanes_of(half, 2 * GROUP), lanes_of(half, 2 * GROUP), lanes_of(length), lanes_of(length), lanes_of(1), whole],
                [lanes_of(length), lanes_of(length + 8), lanes_of(length), whole],
                [shaped(length, pair_width), shaped(length + 8, pair_width), shaped(length, pair_width, kind=bf16), shaped(length, model)],
                [],
            )(normed_one, low, high, fed[pair][4], fed[pair][5], enter[:, lanes], middle)
            mixed.append((gate_pre, states, mixed_low))
        normed_two, normed_two_t = call(
            second_norm_kernel, 1, [SCALARS, whole, fixed((2, model))], [whole, turned],
            [shaped(length, model, kind=bf16), shaped(model, length, kind=bf16)], [pltpu.VMEM((length, model), bf16)],
        )(places, middle, gains)
        normed_two = features(normed_two, True)

        chunk_at = jnp.arange(tensor_size, dtype=jnp.int32) ^ tensor_at
        before = []
        moved = []
        width = 3 * GROUP
        whole_at = pl.BlockSpec((length, model), lambda g, chunks: (0, 0))
        turned_at = pl.BlockSpec((model, length), lambda g, chunks: (0, 0))
        half_at = pl.BlockSpec((half, width), lambda g, chunks: (0, g))
        for at in reversed(range(tensor_size)):
            hold = []
            if len(moved) >= 2:
                before[0], hold = steps([moved[-2]], before[0])

            def kernel(*refs, count=len(before), held=len(hold)):
                sums = refs[8 : 8 + count] if count else (None, None)
                mlp_kernel(*refs[:8], *sums, *refs[8 + count + held :])

            total, normed_grad, low_grad, high_grad = pl.pallas_call(
                kernel,
                grid_spec=pltpu.PrefetchScalarGridSpec(
                    num_scalar_prefetch=1,
                    grid=(mlp_groups,),
                    in_specs=[
                        whole_at, turned_at, whole_at, turned_at,
                    ] + [
                        pl.BlockSpec(
                            (dp_size, 1, block_rows, GROUP),
                            lambda g, chunks, at=at, which=which: (0, chunks[at], 0, which * mlp_groups + g),
                        )
                        for which in range(3)
                    ] + [whole_at] * len(before) + [ANYWHERE] * len(hold),
                    out_specs=[whole_at, whole_at, half_at, half_at],
                    scratch_shapes=[
                        pltpu.VMEM((length, 2 * GROUP), f32), pltpu.VMEM((length, GROUP), bf16),
                        pltpu.VMEM((length, 2 * GROUP), bf16), pltpu.VMEM((length, GROUP), f32),
                    ],
                ),
                out_shape=[shaped(length, model), shaped(length, model)] + [shaped(half, 3 * hidden_chunk, kind=bf16)] * 2,
                compiler_params=PARAMS,
                name="mlp_kernel",
                cost_estimate=pl.CostEstimate(flops=SPANS["mlp_kernel"] * 1150 * 10**6, bytes_accessed=0, transcendentals=0),
            )(chunk_at, normed_two, normed_two_t, cotangent, cot_t, *[mlp_weights] * 3, *before, *hold)
            before = [total, normed_grad]
            moved.append(Scatter(low_grad, high_grad, orders[at % 2], block_rows))
        total, hold = steps([moved[2]], total)
        hidden_out, middle_grad, middle_low, middle_low_t, gain_two = call(
            middle_kernel, 1, [SCALARS, whole, whole, whole, whole, fixed((2, model))],
            [whole, whole, whole, turned, fixed((1, model))],
            [shaped(length, model, kind=bf16), shaped(length, model), shaped(length, model, kind=bf16), shaped(model, length, kind=bf16), shaped(1, model)],
            [pltpu.VMEM((length, model), bf16), pltpu.VMEM((length, model), f32), pltpu.VMEM((length, model), f32)],
            hold=hold,
        )(places, middle, features(total), features(normed_grad), cot_low, gains)
        hidden_out = features(hidden_out, True)

        backs = {}
        out_moved = {}
        gain_two, marks = steps([moved[3], moved[0]], gain_two)
        hold = [gain_two] + marks
        backward = list(reversed(range(pairs)))
        for step, pair in enumerate(backward):
            low, high = out_pairs[pair]
            gate_pre, states, mixed_low = mixed[pair]
            lanes = slice(pair * pair_width, (pair + 1) * pair_width)
            def mix_back(*refs, first=step == 0):
                if first:
                    refs = refs[:10] + (None,) + refs[10:]
                mix_back_kernel(*refs, first=first)

            sums = [normed_grad] if step else []
            normed_grad, local, product, edge, low_grad, high_grad = call(
                mix_back,
                groups,
                [whole, turned, turned, lanes_of(half, 2 * GROUP), lanes_of(half, 2 * GROUP), lanes_of(length), lanes_of(length + 8), lanes_of(length), lanes_of(length), lanes_of(8)] + [whole] * len(sums),
                [whole, lanes_of(length), lanes_of(length), lanes_of(8), lanes_of(half, 2 * GROUP), lanes_of(half, 2 * GROUP)],
                [shaped(length, model), shaped(length, pair_width), shaped(length, pair_width), shaped(8, pair_width), shaped(half, 2 * pair_width, kind=bf16), shaped(half, 2 * pair_width, kind=bf16)],
                [pltpu.VMEM((length, GROUP), f32), pltpu.VMEM((length, GROUP), f32), pltpu.VMEM((length, GROUP), bf16), pltpu.VMEM((length + 8, GROUP), f32)],
                hold=hold,
            )(middle_low, middle_low_t, normed_one_t, low, high, gate_pre, states, mixed_low, fed[pair][2], table[:, lanes], *sums)
            out_moved[pair] = Scatter(low_grad, high_grad, orders[step % 2], block_rows)
            if step == 0:
                edge, marks = steps([moved[1], moved[0]], edge)
                hold = [edge] + marks
            else:
                edge, _ = steps([moved[1]], edge)
            backs[pair] = (local, product, edge)

        def separate(values):
            gate = [values[:, 2 * at * GROUP : (2 * at + 1) * GROUP] for at in range(groups)]
            out = [values[:, (2 * at + 1) * GROUP : (2 * at + 2) * GROUP] for at in range(groups)]
            gate, out = jnp.concatenate(gate, axis=1), jnp.concatenate(out, axis=1)
            return [jnp.concatenate([gate[:, :chunk], out[:, :chunk]], axis=1), jnp.concatenate([gate[:, chunk:], out[:, chunk:]], axis=1)]

        leave = exchange(
            jnp.concatenate([one[2][1:2] for _, one in sorted(backs.items())], axis=1),
            jnp.concatenate([one[2][0:1] for _, one in sorted(backs.items())], axis=1),
            True,
        )
        gate_backs = {}
        mlp_others = {}

        def send_along(step, token):
            other = tensor_size - 1 - step
            values, token = lax.optimization_barrier((moved[step].finish(), token))
            mlp_others[other] = swap_tensor(values, other)
            return token

        leave, hold = steps([moved[2], out_moved[backward[0]]], leave)
        leave = send_along(0, leave)
        for step, pair in enumerate(backward):
            part = slice(2 * pair * local_blocks, 2 * (pair + 1) * local_blocks)
            lanes = slice(pair * pair_width, (pair + 1) * pair_width)
            branch, conv_out, recur_open, inflow = fed[pair][:4]
            local, product, _ = backs[pair]
            gate_backs[pair] = list(
                call(
                    gate_back_kernel,
                    groups,
                    [lanes_of(length), lanes_of(length), lanes_of(1), lanes_of(length + 8)] + [lanes_of(length)] * 3 + [lanes_of(full), blocks_of(), blocks_of(), lanes_of(8)],
                    [lanes_of(length), blocks_of(), blocks_of(), lanes_of(8)],
                    [shaped(length, pair_width), shaped(2 * local_blocks, BLOCK, BLOCK), shaped(2 * local_blocks, BLOCK, BLOCK), shaped(8, pair_width)],
                    [pltpu.VMEM((length, GROUP), bf16)] * 3,
                    hold=hold,
                )(local, product, leave[:, lanes], mixed[pair][1], recur_open, inflow, conv_out, branch, rgates[part], igates[part], table[:, lanes])
            )
            if step == 0:
                token, marks = steps([moved[3], out_moved[backward[1]]], gate_backs[pair][3])
                hold = [token] + marks
                gate_backs[pair][3] = token
            else:
                gate_backs[pair][3], hold = steps([moved[2]], gate_backs[pair][3])
        gate_list = [gate_backs[pair] for pair in range(pairs)]
        heads = jnp.concatenate([one[0][:8] for one in gate_list], axis=1)
        heads = jnp.concatenate(relative(split_lanes(heads, tensor_size), tensor_at), axis=1)
        heads = lax.ppermute(heads, "tensor", [(at + 1, at) for at in range(tensor_size - 1)])
        after = jnp.concatenate(relative(split_lanes(heads, tensor_size), tensor_at), axis=1)
        mlp_others[tensor_size - 1], after = lax.optimization_barrier((mlp_others[tensor_size - 1], after))
        after = send_along(2, send_along(1, after))
        after, marks = steps([out_moved[backward[0]]], after)
        hold = hold + marks
        rgrads = jnp.concatenate([one[1] for one in gate_list], axis=0)
        igrads = jnp.concatenate([one[2] for one in gate_list], axis=0)
        rows = jnp.concatenate([one[3] for one in gate_list], axis=1)
        decay_row = rows[3:4] * (8.0 * jax.nn.sigmoid(-decay_rates))
        rows = jnp.concatenate([rows[4:8], rows[0:3], decay_row], axis=0)
        small_low, small_high = [], []
        if merged:
            small_target = fixed((half, 2 * BLOCK))

            def small_grads(*args, **sizes):
                small_grads_kernel(*args, sub=sub, local_blocks=local_blocks, chunks=tensor_size)
            small_halves = call(
                small_grads, 1, [SCALARS, gate_spec, gate_spec, fixed((kinds, channels))], [small_target] * tensor_size,
                [shaped(half, 2 * BLOCK, kind=bf16)] * tensor_size, [], hold=hold,
            )(places, rgrads, igrads, rows)
            small_low, small_high = small_halves[0::2], small_halves[1::2]
        else:
            gate_grads = jnp.stack([rgrads, igrads], axis=0).reshape(2, tensor_size, local_blocks, dp_size, sub, BLOCK)
            gate_grads = gate_grads.transpose(3, 0, 2, 4, 1, 5).reshape(dp_size, gate_rows, tensor_size * BLOCK)
            gate_grads = jnp.take(gate_grads, natural_at, axis=0)
            rows = rows.reshape(kinds, tensor_size, local_blocks, BLOCK).transpose(0, 2, 1, 3).reshape(1, vector_rows, -1)
            rest = small_rows - gate_rows - vector_rows
            pieces = [
                gate_grads,
                jnp.broadcast_to(rows, (dp_size,) + rows.shape[1:]),
                jnp.zeros((dp_size, rest, tensor_size * BLOCK), f32),
            ]
            small_grads = jnp.concatenate(pieces, axis=1).reshape(dp_size * small_rows, -1).astype(bf16)
            small_own, small_other = jnp.split(small_grads, 2, axis=0)
        if not merged:
            small_moved = Scatter(small_own, small_other, order_one, small_rows)

        in_parts = {}
        for step, pair in enumerate(backward):
            low, high = in_pairs[pair]
            lanes = slice(pair * pair_width, (pair + 1) * pair_width)
            smalls = [small_low[pair], small_high[pair]] if merged else []
            moved_width = pair_width + 2 * BLOCK * merged

            def branch_back(*refs, count=len(smalls)):
                branch_back_kernel(*refs[:7], refs[7 : 7 + count], *refs[7 + count :], groups=groups)

            last = groups - 1
            normed_grad, low_grad, high_grad = call(
                branch_back,
                moved_width // GROUP,
                [lanes_until(length, last), lanes_until(8, last), lanes_until(8, last), turned, lanes_until(half, last), lanes_until(half, last), whole]
                + [fixed((half, GROUP))] * len(smalls),
                [whole, lanes_of(half), lanes_of(half)],
                [shaped(length, model), shaped(half, moved_width, kind=bf16), shaped(half, moved_width, kind=bf16)],
                [pltpu.VMEM((length + 8, GROUP), f32), pltpu.VMEM((length, GROUP), bf16)],
                hold=hold,
            )(gate_backs[pair][0], after[:, lanes], table[:, lanes], normed_one_t, low, high, normed_grad, *smalls)
            in_parts[pair] = Scatter(low_grad, high_grad, orders[step % 2], block_rows)
            if step == 0:
                normed_grad, hold = steps([moved[3], out_moved[backward[1]], out_moved[backward[0]]], normed_grad)
            else:
                normed_grad, hold = steps([out_moved[backward[1]], in_parts[backward[0]], in_parts[backward[1]]], normed_grad)

        hidden_grad, gain_one = call(
            final_kernel, 1, [SCALARS, whole, whole, whole, fixed((2, model))], [whole, fixed((1, model))],
            [shaped(length, model), shaped(1, model)], [pltpu.VMEM((length, model), f32)],
            hold=hold,
        )(places, hidden_low, normed_grad, middle_grad, gains)
        in_list = [in_parts[pair] for pair in backward]
        gain_one, = round_of(in_list, gain_one)
        late = [gain_one]
        gain_parts = jnp.concatenate([gain_one, gain_two], axis=0).reshape(2, dp_size, block_rows)
        if not fast:
            gain_parts = jnp.take(gain_parts, natural_at, axis=1)
        gain_parts = jnp.pad(gain_parts.transpose(1, 0, 2), ((0, 0), (0, 6), (0, BLOCK - block_rows)))
        gain_parts = gain_parts.reshape(8 * dp_size, BLOCK)
        gains_moved = Scatter(gain_parts[: 4 * dp_size], gain_parts[4 * dp_size :], order_one, 8)
        out_parts = [part for pair in range(pairs) for part in separate(out_moved[pair].finish())]
        out_others = {other: swap_tensor(out_parts[other], other) for other in range(tensor_size - 1, 0, -1)}
        mlp_columns = [[((3 * at + which) * GROUP, GROUP) for at in range(mlp_groups)] for which in range(3)]
        mlp_grads = join_parts(moved[-1].finish(), mlp_others, mlp_columns, late)
        far, near = out_others[tensor_size - 1], out_others[tensor_size - 2]
        far, near = round_of(in_list + [gains_moved], far, near)
        out_others.update({tensor_size - 1: far, tensor_size - 2: near})
        round_of([one for one in in_list] + [gains_moved])
        out_columns = [[(0, chunk)], [(chunk, chunk)]]
        gate_grad, out_grad = join_parts(out_parts[0], out_others, out_columns, late)

        def in_chunks(values):
            if not merged:
                return split_lanes(values, 2)
            one, two = values[:, :chunk], values[:, chunk:pair_width]
            small_one, small_two = split_lanes(values[:, pair_width:], 2)
            return [jnp.concatenate([one, small_one], axis=1), jnp.concatenate([two, small_two], axis=1)]

        in_sum, in_far = join_tensor([part for pair in range(pairs) for part in in_chunks(in_parts[pair].finish())])
        gain_sum = gains_moved.finish()
        gain_sum = sum(spread_tensor(gain_sum)[1:], gain_sum)
        gain_rows = block_rows // tensor_size
        gain_sum = lax.dynamic_slice(gain_sum, (0, tensor_at * gain_rows), (2, gain_rows)).T

        hidden_grad = features(hidden_grad, True)
        if merged:
            in_sum, small_sum = in_sum[:, :chunk], in_sum[:, chunk:]
        else:
            small_sum, _ = join_tensor(split_lanes(small_moved.finish(), tensor_size))

        gate_sum = small_sum[:gate_rows].reshape(2, local_blocks, sub, BLOCK).transpose(0, 2, 1, 3)
        vector_sum = lax.dynamic_slice(small_sum, (gate_rows, dp_at * sub), (vector_rows, sub))
        vector_sum = vector_sum.reshape(kinds, local_blocks, sub)

        return (
            hidden_out,
            hidden_grad,
            gain_sum,
            in_sum,
            gate_grad,
            out_grad,
            gate_sum[1],
            gate_sum[0],
            vector_sum[:CONV].transpose(2, 0, 1),
            vector_sum[4].T,
            vector_sum[5].T,
            vector_sum[6].T,
            vector_sum[7].T,
            mlp_grads[0],
            mlp_grads[1],
            mlp_grads[2],
        )

    return per_device


def solution(mesh):
    rows = P(("dp", "tensor"), None)
    matrix = P("dp", "tensor")
    gate = P("dp", "tensor", None)
    kernel = P("dp", None, "tensor")
    placed = (rows, rows, P("dp", None), matrix, matrix, matrix, gate, gate, kernel) + (matrix,) * 7
    made = (rows, rows, rows, matrix, matrix, matrix, gate, gate, kernel) + (matrix,) * 7
    return jax.shard_map(
        make_per_device(mesh.shape["dp"], mesh.shape["tensor"]),
        mesh=mesh,
        in_specs=placed,
        out_specs=made,
        check_vma=False,
    )
```

profile of v0, /device:TPU:0, one launch (start us, length us, event | category | flops | bytes accessed | tf_op | source)
XLA Modules:
  0.0 430.6 jit_solution(10373966490799368377)
XLA Ops:
  10.0 3.1 collective-permute-start
  22.3 3.8 collective-permute-done.1
  26.2 10.5 %collective-permute-start.6 = (bf16[128,768]{1,0:T(8,128)(2,1)S(1)}, bf16[128,768]{1,0:T(8,128)(2,1)S(1)}, u32[]{:S(2)}, u32[]{:S(2)}) collective-permute-start(bf16[128,768]{1,0:T(8,128)(2,1)S(1)} %constant_dynamic-update-slice_fusion), channel_id=1, source_target_pairs={{0,1},{1,0},{2,3},{3,2},{4,5},{5,4},{6,7},{7,6},{8,9},{9,8},{10,11... | collective-permute-start | bytes 589832 | tf_op jit(solution)/shard_map/ppermute | solution.py:588
  43.8 3.3 collective-permute-done.6
  47.2 10.2 %collective-permute-done.7 = bf16[128,768]{1,0:T(8,128)(2,1)S(1)} collective-permute-done((bf16[128,768]{1,0:T(8,128)(2,1)S(1)}, bf16[128,768]{1,0:T(8,128)(2,1)S(1)}, u32[]{:S(2)}, u32[]{:S(2)}) %collective-permute-start.7) | collective-permute-done | bytes 196640 | tf_op jit(solution)/shard_map/ppermute | solution.py:588
  62.1 8.4 %collective-permute-done.12 = bf16[128,1536]{1,0:T(8,128)(2,1)S(1)} collective-permute-done((bf16[128,1536]{1,0:T(8,128)(2,1)S(1)}, bf16[128,1536]{1,0:T(8,128)(2,1)S(1)}, u32[]{:S(2)}, u32[]{:S(2)}) %collective-permute-start.12) | collective-permute-done | bytes 393248 | tf_op jit(solution)/shard_map/ppermute | solution.py:585
  70.6 17.3 %collective-permute-done.11 = bf16[128,1536]{1,0:T(8,128)(2,1)S(1)} collective-permute-done((bf16[128,1536]{1,0:T(8,128)(2,1)S(1)}, bf16[128,1536]{1,0:T(8,128)(2,1)S(1)}, u32[]{:S(2)}, u32[]{:S(2)}) %collective-permute-start.11) | collective-permute-done | bytes 393248 | tf_op jit(solution)/shard_map/ppermute | solution.py:585
  96.3 2.9 norm_kernel.1
  99.3 12.4 %mix_in_kernel.2 = (f32[528,768]{1,0:T(8,128)S(1)}, f32[512,768]{1,0:T(8,128)S(1)}, f32[512,768]{1,0:T(8,128)S(1)}, f32[512,768]{1,0:T(8,128)S(1)}, f32[512,768]{1,0:T(8,128)S(1)}, /*index=5*/f32[512,768]{1,0:T(8,128)S(1)}) custom-call(bf16[528,1024]{1,0:T(8,128)(2,1)S(1)} %get-tuple-element.196.refs_0_, ...), custom_call_target="tpu_custom_call" | custom-call | flops 16099999744 | tf_op jit(solution)/shard_map/mix_in_kernel/pallas_call | solution.py:573
  116.5 9.9 %collective-permute-done.16 = bf16[256,1536]{1,0:T(8,128)(2,1)S(1)} collective-permute-done((bf16[256,1536]{1,0:T(8,128)(2,1)S(1)}, bf16[256,1536]{1,0:T(8,128)(2,1)S(1)}, u32[]{:S(2)}, u32[]{:S(2)}) %collective-permute-start.16) | collective-permute-done | bytes 786464 | tf_op jit(solution)/shard_map/ppermute | solution.py:585
  127.2 11.4 %mix_in_kernel.3 = (f32[528,768]{1,0:T(8,128)S(1)}, f32[512,768]{1,0:T(8,128)S(1)}, f32[512,768]{1,0:T(8,128)S(1)}, f32[512,768]{1,0:T(8,128)S(1)}, f32[512,768]{1,0:T(8,128)S(1)}, /*index=5*/f32[512,768]{1,0:T(8,128)S(1)}) custom-call(bf16[528,1024]{1,0:T(8,128)(2,1)S(1)} %get-tuple-element.196.refs_0_, ...), custom_call_target="tpu_custom_call" | custom-call | flops 16099999744 | tf_op jit(solution)/shard_map/mix_in_kernel/pallas_call | solution.py:573
  141.0 6.9 %collective-permute-start.18 = (f32[2,1536]{1,0:T(2,128)S(1)}, f32[2,1536]{1,0:T(2,128)S(1)}, u32[]{:S(2)}, u32[]{:S(2)}) collective-permute-start(f32[2,1536]{1,0:T(2,128)S(1)} %maximum_maximum_fusion), channel_id=1, source_target_pairs={{0,1},{1,0},{2,3},{3,2},{4,5},{5,4},{6,7},{7,6},{8,9},{9,8},{10,11... | collective-permute-start | bytes 36872 | tf_op jit(solution)/shard_map/ppermute | solution.py:588
  147.8 3.7 collective-permute-start.19
  153.9 3.1 collective-permute-done.20
  157.2 6.4 %mix_out_kernel.2 = (f32[512,768]{1,0:T(8,128)S(1)}, f32[520,768]{1,0:T(8,128)S(1)}, bf16[512,768]{1,0:T(8,128)(2,1)S(1)}, f32[512,1024]{1,0:T(8,128)S(1)}) custom-call(bf16[528,1024]{1,0:T(8,128)(2,1)S(1)} %get-tuple-element.196.refs_0_, bf16[512,1536]{1,0:T(8,128)(2,1)S(1)} %pad_maximum_fusion.1.refs_1_.refs_3_, ...), custom_call_target="tpu_custom_call" | custom-call | flops 11500000256 | tf_op jit(solution)/shard_map/mix_out_kernel/pallas_call | solution.py:573
  164.8 6.4 %mix_out_kernel.3 = (f32[512,768]{1,0:T(8,128)S(1)}, f32[520,768]{1,0:T(8,128)S(1)}, bf16[512,768]{1,0:T(8,128)(2,1)S(1)}, f32[512,1024]{1,0:T(8,128)S(1)}) custom-call(bf16[528,1024]{1,0:T(8,128)(2,1)S(1)} %get-tuple-element.196.refs_0_, bf16[512,1536]{1,0:T(8,128)(2,1)S(1)} %pad_maximum_fusion.refs_1_.refs_3_, ...), custom_call_target="tpu_custom_call" | custom-call | flops 11500000256 | tf_op jit(solution)/shard_map/mix_out_kernel/pallas_call | solution.py:573
  185.5 14.2 %mlp_kernel.4 = (f32[512,1024]{1,0:T(8,128)S(1)}, f32[512,1024]{1,0:T(8,128)S(1)}, bf16[512,2304]{1,0:T(8,128)(2,1)S(1)}, bf16[512,2304]{1,0:T(8,128)(2,1)S(1)}) custom-call(s32[4]{0:T(128)S(1)} %iota_xor_fusion.refs_0_, bf16[512,1024]{1,0:T(8,128)(2,1)S(1)} %copy-done.29, bf16[1024,512]{1,0:T(8,128)(2,1)S(1)} %copy-done.31, ...), custom_call_target="tpu_custom_call" | custom-call | flops 19549999104 | tf_op jit(solution)/shard_map/mlp_kernel/pallas_call | solution.py:914
  199.8 14.7 %mlp_kernel.5 = (f32[512,1024]{1,0:T(8,128)S(1)}, f32[512,1024]{1,0:T(8,128)S(1)}, bf16[512,2304]{1,0:T(8,128)(2,1)S(1)}, bf16[512,2304]{1,0:T(8,128)(2,1)S(1)}) custom-call(s32[4]{0:T(128)S(1)} %iota_xor_fusion.refs_0_, bf16[512,1024]{1,0:T(8,128)(2,1)S(1)} %copy-done.29, bf16[1024,512]{1,0:T(8,128)(2,1)S(1)} %copy-done.31, ...), custom_call_target="tpu_custom_call" | custom-call | flops 19549999104 | tf_op jit(solution)/shard_map/mlp_kernel/pallas_call | solution.py:914
  217.1 14.2 %mlp_kernel.6 = (f32[512,1024]{1,0:T(8,128)S(1)}, f32[512,1024]{1,0:T(8,128)S(1)}, bf16[512,2304]{1,0:T(8,128)(2,1)S(1)}, bf16[512,2304]{1,0:T(8,128)(2,1)S(1)}) custom-call(s32[4]{0:T(128)S(1)} %iota_xor_fusion.refs_0_, bf16[512,1024]{1,0:T(8,128)(2,1)S(1)} %copy-done.29, bf16[1024,512]{1,0:T(8,128)(2,1)S(1)} %copy-done.31, ...), custom_call_target="tpu_custom_call" | custom-call | flops 19549999104 | tf_op jit(solution)/shard_map/mlp_kernel/pallas_call | solution.py:914
  233.9 14.5 %mlp_kernel.7 = (f32[512,1024]{1,0:T(8,128)S(1)}, f32[512,1024]{1,0:T(8,128)S(1)}, bf16[512,2304]{1,0:T(8,128)(2,1)S(1)}, bf16[512,2304]{1,0:T(8,128)(2,1)S(1)}) custom-call(s32[4]{0:T(128)S(1)} %iota_xor_fusion.refs_0_, bf16[512,1024]{1,0:T(8,128)(2,1)S(1)} %copy-done.29, bf16[1024,512]{1,0:T(8,128)(2,1)S(1)} %copy-done.31, ...), custom_call_target="tpu_custom_call" | custom-call | flops 19549999104 | tf_op jit(solution)/shard_map/mlp_kernel/pallas_call | solution.py:914
  252.1 6.1 %middle_kernel.1 = (bf16[512,1024]{1,0:T(8,128)(2,1)}, f32[512,1024]{1,0:T(8,128)S(1)}, bf16[512,1024]{1,0:T(8,128)(2,1)S(1)}, bf16[1024,512]{1,0:T(8,128)(2,1)S(1)}, f32[1,1024]{1,0:T(1,128)S(1)}) custom-call(s32[8]{0:T(128)S(1)} %broadcast_xor_fusion.refs_0_, f32[512,1024]{1,0:T(8,128)S(1)} %copy-done.38, f32[512,1024]{1,0:T(8,128)S(1)} %get-tuple-element.230.refs_2_, ...), custom_call_target="tpu_custom_call" | custom-call | flops 13799999488 | tf_op jit(solution)/shard_map/middle_kernel/pallas_call | solution.py:573
  262.0 3.4 add_convert_fusion
  266.3 13.7 %mix_back.2 = (f32[512,1024]{1,0:T(8,128)S(1)}, f32[512,768]{1,0:T(8,128)S(1)}, f32[512,768]{1,0:T(8,128)S(1)}, f32[8,768]{1,0:T(8,128)S(1)}, bf16[512,1536]{1,0...) custom-call(bf16[512,1024]{1,0:T(8,128)(2,1)S(1)} %get-tuple-element.236.refs_0_, ...), custom_call_target="tpu_custom_call" | custom-call | flops 20700000256 | tf_op jit(solution)/shard_map/mix_back/pallas_call | solution.py:573
  287.4 13.6 %mix_back.3 = (f32[512,1024]{1,0:T(8,128)S(1)}, f32[512,768]{1,0:T(8,128)S(1)}, f32[512,768]{1,0:T(8,128)S(1)}, f32[8,768]{1,0:T(8,128)S(1)}, bf16[512,1536]{1,0...) custom-call(bf16[512,1024]{1,0:T(8,128)(2,1)S(1)} %get-tuple-element.236.refs_0_, ...), custom_call_target="tpu_custom_call" | custom-call | flops 20700000256 | tf_op jit(solution)/shard_map/mix_back/pallas_call | solution.py:573
  316.1 8.4 %gate_back_kernel.2 = (f32[512,768]{1,0:T(8,128)S(1)}, f32[6,128,128]{2,1,0:T(8,128)S(1)}, f32[6,128,128]{2,1,0:T(8,128)S(1)}, f32[8,768]{1,0:T(8,128)S(1)}) custom-call(f32[512,768]{1,0:T(8,128)S(1)} %copy-done.71, f32[512,768]{1,0:T(8,128)S(1)} %copy-done.73, f32[1,768]{1,0:T(1,128)S(1)} %get-tuple-element.484.refs_2_, f32[520,768]{1,0:T(8,128)S(1)} %copy-done.45, ...), custom_call_target="tpu_custom_call" | custom-call | flops 12650000384 | tf_op jit(solution)/shard_map/gate_back_kernel/pallas_call | solution.py:573
  324.5 2.9 collective-permute-start.39
  333.4 8.6 %gate_back_kernel.3 = (f32[512,768]{1,0:T(8,128)S(1)}, f32[6,128,128]{2,1,0:T(8,128)S(1)}, f32[6,128,128]{2,1,0:T(8,128)S(1)}, f32[8,768]{1,0:T(8,128)S(1)}) custom-call(f32[512,768]{1,0:T(8,128)S(1)} %get-tuple-element.260.refs_0_, f32[512,768]{1,0:T(8,128)S(1)} %copy-done.62, f32[1,768]{1,0:T(1,128)S(1)} %get-tuple-element.485.refs_2_, ...), custom_call_target="tpu_custom_call" | custom-call | flops 12650000384 | tf_op jit(solution)/shard_map/gate_back_kernel/pallas_call | solution.py:573
  349.9 3.9 collective-permute-start.63
  356.9 5.3 %branch_back.2 = (f32[512,1024]{1,0:T(8,128)S(1)}, bf16[512,1024]{1,0:T(8,128)(2,1)S(1)}, bf16[512,1024]{1,0:T(8,128)(2,1)S(1)}) custom-call(f32[512,768]{1,0:T(8,128)S(1)} %get-tuple-element.291.refs_0_, f32[8,768]{1,0:T(8,128)S(1)} %get-tuple-element.448.refs_1_, f32[8,768]{1,0:T(8,128)S(1)} %copy-done.18, bf16[1024,512]{1,0:T(8,128)(2,1)S(1)} %copy-done.40, ...), custom_call_target="tpu_custom_call" | custom-call | flops 9200000000 | tf_op jit(solution)/shard_map/branch_back/pallas_call | solution.py:573
  363.7 4.0 collective-permute-done.41
  370.2 4.4 %branch_back.3 = (f32[512,1024]{1,0:T(8,128)S(1)}, bf16[512,1024]{1,0:T(8,128)(2,1)S(1)}, bf16[512,1024]{1,0:T(8,128)(2,1)S(1)}) custom-call(f32[512,768]{1,0:T(8,128)S(1)} %get-tuple-element.286.refs_0_, f32[8,768]{1,0:T(8,128)S(1)} %get-tuple-element.449.refs_1_, f32[8,768]{1,0:T(8,128)S(1)} %copy-done.16, bf16[1024,512]{1,0:T(8,128)(2,1)S(1)} %copy-done.40, ...), custom_call_target="tpu_custom_call" | custom-call | flops 9200000000 | tf_op jit(solution)/shard_map/branch_back/pallas_call | solution.py:573
  383.5 5.5 %final_kernel.1 = (f32[512,1024]{1,0:T(8,128)}, f32[1,1024]{1,0:T(1,128)S(1)}) custom-call(s32[8]{0:T(128)S(1)} %broadcast_xor_fusion.refs_0_, bf16[512,1024]{1,0:T(8,128)(2,1)S(1)} %copy-done.34, f32[512,1024]{1,0:T(8,128)S(1)} %get-tuple-element.319.refs_2_, f32[512,1024]{1,0:T(8,128)S(1)} %copy-done.42, ...), custom_call_target="tpu_custom_call" | custom-call | flops 11500000256 | tf_op jit(solution)/shard_map/final_kernel/pallas_call | solution.py:573
  (502 shorter events, 156.9 us)
Async XLA Ops:
  7.3 173.2 %all-gather.3.cloned.1.call-start = ((), (), s32[]{:S(2)}) async-start(), calls=%async_computation | async-start | bytes 19464192 | tf_op jit(solution)/shard_map/all_gather | solution.py:805
  26.2 21.0 %collective-permute-start.6 = (bf16[128,768]{1,0:T(8,128)(2,1)S(1)}, bf16[128,768]{1,0:T(8,128)(2,1)S(1)}, u32[]{:S(2)}, u32[]{:S(2)}) collective-permute-start(bf16[128,768]{1,0:T(8,128)(2,1)S(1)} %constant_dynamic-update-slice_fusion), channel_id=1, source_target_pairs={{0,1},{1,0},{2,3},{3,2},{4,5},{5,4},{6,7},{7,6},{8,9},{9,8},{10,11... | collective-permute-start | bytes 589832 | tf_op jit(solution)/shard_map/ppermute | solution.py:588
  36.7 20.7 %collective-permute-start.7 = (bf16[128,768]{1,0:T(8,128)(2,1)S(1)}, bf16[128,768]{1,0:T(8,128)(2,1)S(1)}, u32[]{:S(2)}, u32[]{:S(2)}) collective-permute-start(bf16[128,768]{1,0:T(8,128)(2,1)S(1)} %constant_dynamic-update-slice_fusion), channel_id=1, source_target_pairs={{0,2},{1,3},{2,0},{3,1},{4,6},{5,7},{6,4},{7,5},{8,10},{9,11},{10,... | collective-permute-start | bytes 589832 | tf_op jit(solution)/shard_map/ppermute | solution.py:588
  39.4 18.0 %collective-permute-start.8 = (bf16[128,768]{1,0:T(8,128)(2,1)S(1)}, bf16[128,768]{1,0:T(8,128)(2,1)S(1)}, u32[]{:S(2)}, u32[]{:S(2)}) collective-permute-start(bf16[128,768]{1,0:T(8,128)(2,1)S(1)} %constant_dynamic-update-slice_fusion), channel_id=1, source_target_pairs={{0,3},{1,2},{2,1},{3,0},{4,7},{5,6},{6,5},{7,4},{8,11},{9,10},{10,... | collective-permute-start | bytes 589832 | tf_op jit(solution)/shard_map/ppermute | solution.py:588
  40.8 16.6 %collective-permute-start.5 = (bf16[128,1024]{1,0:T(8,128)(2,1)S(1)}, bf16[128,1024]{1,0:T(8,128)(2,1)S(1)}, u32[]{:S(2)}, u32[]{:S(2)}) collective-permute-start(bf16[128,1024]{1,0:T(8,128)(2,1)S(1)} %pad_maximum_fusion.12), channel_id=1, source_target_pairs={{0,16},{4,20},{8,24},{12,28},{16,0},{20,4},{24,8},{28,12},{1,17},{... | collective-permute-start | bytes 786440 | tf_op jit(solution)/shard_map/ppermute | solution.py:585
  59.1 28.8 %collective-permute-start.10 = (bf16[256,1024]{1,0:T(8,128)(2,1)S(1)}, bf16[256,1024]{1,0:T(8,128)(2,1)S(1)}, u32[]{:S(2)}, u32[]{:S(2)}) collective-permute-start(bf16[256,1024]{1,0:T(8,128)(2,1)S(1)} %pad_maximum_fusion.10), channel_id=1, source_target_pairs={{0,8},{4,12},{8,0},{12,4},{16,24},{20,28},{24,16},{28,20},{1,9},{5... | collective-permute-start | bytes 1572872 | tf_op jit(solution)/shard_map/ppermute | solution.py:585
  60.5 27.4 %collective-permute-start.9 = (bf16[256,1024]{1,0:T(8,128)(2,1)S(1)}, bf16[256,1024]{1,0:T(8,128)(2,1)S(1)}, u32[]{:S(2)}, u32[]{:S(2)}) collective-permute-start(bf16[256,1024]{1,0:T(8,128)(2,1)S(1)} %pad_maximum_fusion.9), channel_id=1, source_target_pairs={{0,16},{4,20},{8,24},{12,28},{16,0},{20,4},{24,8},{28,12},{1,17},{... | collective-permute-start | bytes 1572872 | tf_op jit(solution)/shard_map/ppermute | solution.py:585
  61.3 26.6 %collective-permute-start.11 = (bf16[128,1536]{1,0:T(8,128)(2,1)S(1)}, bf16[128,1536]{1,0:T(8,128)(2,1)S(1)}, u32[]{:S(2)}, u32[]{:S(2)}) collective-permute-start(bf16[128,1536]{1,0:T(8,128)(2,1)S(1)} %slice_dynamic-update-slice_fusion.4), channel_id=1, source_target_pairs={{0,8},{4,12},{8,0},{12,4},{16,24},{20,28},{24,16},{28,20},{1,9},{5... | collective-permute-start | bytes 1179656 | tf_op jit(solution)/shard_map/ppermute | solution.py:585
  90.8 35.5 %collective-permute-start.16 = (bf16[256,1536]{1,0:T(8,128)(2,1)S(1)}, bf16[256,1536]{1,0:T(8,128)(2,1)S(1)}, u32[]{:S(2)}, u32[]{:S(2)}) collective-permute-start(bf16[256,1536]{1,0:T(8,128)(2,1)S(1)} %pad_maximum_fusion.5), channel_id=1, source_target_pairs={{0,8},{4,12},{8,0},{12,4},{16,24},{20,28},{24,16},{28,20},{1,9},{5... | collective-permute-start | bytes 2359304 | tf_op jit(solution)/shard_map/ppermute | solution.py:585
  91.3 35.8 %collective-permute-start.15 = (bf16[256,1536]{1,0:T(8,128)(2,1)S(1)}, bf16[256,1536]{1,0:T(8,128)(2,1)S(1)}, u32[]{:S(2)}, u32[]{:S(2)}) collective-permute-start(bf16[256,1536]{1,0:T(8,128)(2,1)S(1)} %pad_maximum_fusion.4), channel_id=1, source_target_pairs={{0,16},{4,20},{8,24},{12,28},{16,0},{20,4},{24,8},{28,12},{1,17},{... | collective-permute-start | bytes 2359304 | tf_op jit(solution)/shard_map/ppermute | solution.py:585
  199.7 15.5 %collective-permute-start.22 = (bf16[512,2304]{1,0:T(8,128)(2,1)S(1)}, bf16[512,2304]{1,0:T(8,128)(2,1)S(1)}, u32[]{:S(2)}, u32[]{:S(2)}) collective-permute-start(bf16[512,2304]{1,0:T(8,128)(2,1)S(1)} %get-tuple-element.214), channel_id=1, source_target_pairs={{0,4},{4,0},{8,12},{12,8},{16,20},{20,16},{24,28},{28,24},{1,5},{5... | collective-permute-start | bytes 7077896 | tf_op jit(solution)/shard_map/ppermute | solution.py:585
  214.5 16.9 %collective-permute-start.24 = (bf16[512,2304]{1,0:T(8,128)(2,1)S(1)}, bf16[512,2304]{1,0:T(8,128)(2,1)S(1)}, u32[]{:S(2)}, u32[]{:S(2)}) collective-permute-start(bf16[512,2304]{1,0:T(8,128)(2,1)S(1)} %get-tuple-element.223), channel_id=1, source_target_pairs={{0,4},{4,0},{8,12},{12,8},{16,20},{20,16},{24,28},{28,24},{1,5},{5... | collective-permute-start | bytes 7077896 | tf_op jit(solution)/shard_map/ppermute | solution.py:585
  215.7 43.8 %collective-permute-start.25 = (bf16[256,2304]{1,0:T(8,128)(2,1)S(1)}, bf16[256,2304]{1,0:T(8,128)(2,1)}, u32[]{:S(2)}, u32[]{:S(2)}) collective-permute-start(bf16[256,2304]{1,0:T(8,128)(2,1)S(1)} %add_convert_fusion.7.refs_10_), channel_id=1, source_target_pairs={{0,8},{4,12},{8,0},{12,4},{16,24},{20,28},{24,16},{28,20},{1,9},{5... | collective-permute-start | bytes 3538952 | tf_op jit(solution)/shard_map/ppermute | solution.py:585
  231.4 17.8 %collective-permute-start.23 = (bf16[512,2304]{1,0:T(8,128)(2,1)S(1)}, bf16[512,2304]{1,0:T(8,128)(2,1)S(1)}, u32[]{:S(2)}, u32[]{:S(2)}) collective-permute-start(bf16[512,2304]{1,0:T(8,128)(2,1)S(1)} %get-tuple-element.222), channel_id=1, source_target_pairs={{0,4},{4,0},{8,12},{12,8},{16,20},{20,16},{24,28},{28,24},{1,5},{5... | collective-permute-start | bytes 7077896 | tf_op jit(solution)/shard_map/ppermute | solution.py:585
  233.1 46.9 %collective-permute-start.28 = (bf16[256,2304]{1,0:T(8,128)(2,1)S(1)}, bf16[256,2304]{1,0:T(8,128)(2,1)}, u32[]{:S(2)}, u32[]{:S(2)}) collective-permute-start(bf16[256,2304]{1,0:T(8,128)(2,1)S(1)} %get-tuple-element.363.refs_10_), channel_id=1, source_target_pairs={{0,16},{4,20},{8,24},{12,28},{16,0},{20,4},{24,8},{28,12},{1,17},{... | collective-permute-start | bytes 3538952 | tf_op jit(solution)/shard_map/ppermute | solution.py:585
  250.5 60.1 %collective-permute-start.30 = (bf16[256,2304]{1,0:T(8,128)(2,1)S(1)}, bf16[256,2304]{1,0:T(8,128)(2,1)}, u32[]{:S(2)}, u32[]{:S(2)}) collective-permute-start(bf16[256,2304]{1,0:T(8,128)(2,1)S(1)} %add_convert_fusion.5.refs_6_), channel_id=1, source_target_pairs={{0,8},{4,12},{8,0},{12,4},{16,24},{20,28},{24,16},{28,20},{1,9},{5... | collective-permute-start | bytes 3538952 | tf_op jit(solution)/shard_map/ppermute | solution.py:585
  260.7 22.4 %collective-permute-start.27 = (bf16[128,2304]{1,0:T(8,128)(2,1)S(1)}, bf16[128,2304]{1,0:T(8,128)(2,1)S(1)}, u32[]{:S(2)}, u32[]{:S(2)}) collective-permute-start(bf16[128,2304]{1,0:T(8,128)(2,1)S(1)} %add_convert_fusion.23.refs_12_), channel_id=1, source_target_pairs={{0,16},{4,20},{8,24},{12,28},{16,0},{20,4},{24,8},{28,12},{1,17},{... | collective-permute-start | bytes 1769480 | tf_op jit(solution)/shard_map/ppermute | solution.py:585
  265.5 59.1 %collective-permute-start.36 = (bf16[256,2304]{1,0:T(8,128)(2,1)S(1)}, bf16[256,2304]{1,0:T(8,128)(2,1)}, u32[]{:S(2)}, u32[]{:S(2)}) collective-permute-start(bf16[256,2304]{1,0:T(8,128)(2,1)S(1)} %get-tuple-element.361.refs_11_), channel_id=1, source_target_pairs={{0,16},{4,20},{8,24},{12,28},{16,0},{20,4},{24,8},{28,12},{1,17},{... | collective-permute-start | bytes 3538952 | tf_op jit(solution)/shard_map/ppermute | solution.py:585
  281.8 19.2 %collective-permute-start.31 = (bf16[128,2304]{1,0:T(8,128)(2,1)S(1)}, bf16[128,2304]{1,0:T(8,128)(2,1)S(1)}, u32[]{:S(2)}, u32[]{:S(2)}) collective-permute-start(bf16[128,2304]{1,0:T(8,128)(2,1)S(1)} %add_convert_fusion.22.refs_12_), channel_id=1, source_target_pairs={{0,8},{4,12},{8,0},{12,4},{16,24},{20,28},{24,16},{28,20},{1,9},{5... | collective-permute-start | bytes 1769480 | tf_op jit(solution)/shard_map/ppermute | solution.py:585
  282.7 30.2 %collective-permute-start.29 = (bf16[512,1536]{1,0:T(8,128)(2,1)S(1)}, bf16[512,1536]{1,0:T(8,128)(2,1)}, u32[]{:S(2)}, u32[]{:S(2)}) collective-permute-start(bf16[512,1536]{1,0:T(8,128)(2,1)S(1)} %get-tuple-element.262), channel_id=1, source_target_pairs={{0,4},{4,0},{8,12},{12,8},{16,20},{20,16},{24,28},{28,24},{1,5},{5... | collective-permute-start | bytes 4718600 | tf_op jit(solution)/shard_map/ppermute | solution.py:585
  308.6 21.4 %collective-permute-start.35 = (bf16[512,1536]{1,0:T(8,128)(2,1)S(1)}, bf16[512,1536]{1,0:T(8,128)(2,1)}, u32[]{:S(2)}, u32[]{:S(2)}) collective-permute-start(bf16[512,1536]{1,0:T(8,128)(2,1)S(1)} %get-tuple-element.271), channel_id=1, source_target_pairs={{0,4},{4,0},{8,12},{12,8},{16,20},{20,16},{24,28},{28,24},{1,5},{5... | collective-permute-start | bytes 4718600 | tf_op jit(solution)/shard_map/ppermute | solution.py:585
  311.9 30.1 %collective-permute-start.38 = (bf16[128,2304]{1,0:T(8,128)(2,1)S(1)}, bf16[128,2304]{1,0:T(8,128)(2,1)}, u32[]{:S(2)}, u32[]{:S(2)}) collective-permute-start(bf16[128,2304]{1,0:T(8,128)(2,1)S(1)} %add_convert_fusion.19.refs_11_), channel_id=1, source_target_pairs={{0,16},{4,20},{8,24},{12,28},{16,0},{20,4},{24,8},{28,12},{1,17},{... | collective-permute-start | bytes 1769480 | tf_op jit(solution)/shard_map/ppermute | solution.py:585
  314.9 38.9 %collective-permute-start.37 = (bf16[256,1536]{1,0:T(8,128)(2,1)S(1)}, bf16[256,1536]{1,0:T(8,128)(2,1)}, u32[]{:S(2)}, u32[]{:S(2)}) collective-permute-start(bf16[256,1536]{1,0:T(8,128)(2,1)S(1)} %get-tuple-element.365.refs_12_), channel_id=1, source_target_pairs={{0,16},{4,20},{8,24},{12,28},{16,0},{20,4},{24,8},{28,12},{1,17},{... | collective-permute-start | bytes 2359304 | tf_op jit(solution)/shard_map/ppermute | solution.py:585
  324.5 25.3 %collective-permute-start.39 = (bf16[128,2304]{1,0:T(8,128)(2,1)S(1)}, bf16[128,2304]{1,0:T(8,128)(2,1)S(1)}, u32[]{:S(2)}, u32[]{:S(2)}) collective-permute-start(bf16[128,2304]{1,0:T(8,128)(2,1)S(1)} %add_convert_fusion.20.refs_13_), channel_id=1, source_target_pairs={{0,3},{1,2},{2,1},{3,0},{4,7},{5,6},{6,5},{7,4},{8,11},{9,10},{10,... | collective-permute-start | bytes 1769480 | tf_op jit(solution)/shard_map/ppermute | solution.py:588
  328.8 33.3 %collective-permute-start.43 = (bf16[128,2304]{1,0:T(8,128)(2,1)S(1)}, bf16[128,2304]{1,0:T(8,128)(2,1)S(1)}, u32[]{:S(2)}, u32[]{:S(2)}) collective-permute-start(bf16[128,2304]{1,0:T(8,128)(2,1)S(1)} %add_convert_fusion.18.refs_12_), channel_id=1, source_target_pairs={{0,8},{4,12},{8,0},{12,4},{16,24},{20,28},{24,16},{28,20},{1,9},{5... | collective-permute-start | bytes 1769480 | tf_op jit(solution)/shard_map/ppermute | solution.py:585
  342.9 20.8 %collective-permute-start.42 = (bf16[256,1536]{1,0:T(8,128)(2,1)S(1)}, bf16[256,1536]{1,0:T(8,128)(2,1)S(1)}, u32[]{:S(2)}, u32[]{:S(2)}) collective-permute-start(bf16[256,1536]{1,0:T(8,128)(2,1)S(1)} %add_convert_fusion.10.refs_13_), channel_id=1, source_target_pairs={{0,8},{4,12},{8,0},{12,4},{16,24},{20,28},{24,16},{28,20},{1,9},{5... | collective-permute-start | bytes 2359304 | tf_op jit(solution)/shard_map/ppermute | solution.py:585
  349.9 44.2 %collective-permute-start.63 = (bf16[128,2304]{1,0:T(8,128)(2,1)S(1)}, bf16[128,2304]{1,0:T(8,128)(2,1)S(1)}, u32[]{:S(2)}, u32[]{:S(2)}) collective-permute-start(bf16[128,2304]{1,0:T(8,128)(2,1)S(1)} %add_convert_fusion.16.refs_4_.refs_9_), channel_id=1, source_target_pairs={{0,1},{1,0},{2,3},{3,2},{4,5},{5,4},{6,7},{7,6},{8,9},{9,8},{10,11... | collective-permute-start | bytes 1769480 | tf_op jit(solution)/shard_map/ppermute | solution.py:588
  353.8 41.6 %collective-permute-start.64 = (bf16[128,2304]{1,0:T(8,128)(2,1)S(1)}, bf16[128,2304]{1,0:T(8,128)(2,1)S(1)}, u32[]{:S(2)}, u32[]{:S(2)}) collective-permute-start(bf16[128,2304]{1,0:T(8,128)(2,1)S(1)} %copy-done.101), channel_id=1, source_target_pairs={{0,2},{1,3},{2,0},{3,1},{4,6},{5,7},{6,4},{7,5},{8,10},{9,11},{10,... | collective-permute-start | bytes 1769480 | tf_op jit(solution)/shard_map/ppermute | solution.py:588
  362.2 18.1 %collective-permute-start.45 = (bf16[512,1024]{1,0:T(8,128)(2,1)S(1)}, bf16[512,1024]{1,0:T(8,128)(2,1)S(1)}, u32[]{:S(2)}, u32[]{:S(2)}) collective-permute-start(bf16[512,1024]{1,0:T(8,128)(2,1)S(1)} %get-tuple-element.315), channel_id=1, source_target_pairs={{0,4},{4,0},{8,12},{12,8},{16,20},{20,16},{24,28},{28,24},{1,5},{5... | collective-permute-start | bytes 3145736 | tf_op jit(solution)/shard_map/ppermute | solution.py:585
  377.6 19.0 %collective-permute-start.52 = (bf16[128,768]{1,0:T(8,128)(2,1)S(1)}, bf16[128,768]{1,0:T(8,128)(2,1)S(1)}, u32[]{:S(2)}, u32[]{:S(2)}) collective-permute-start(bf16[128,768]{1,0:T(8,128)(2,1)S(1)} %get-tuple-element.441), channel_id=1, source_target_pairs={{0,3},{1,2},{2,1},{3,0},{4,7},{5,6},{6,5},{7,4},{8,11},{9,10},{10,... | collective-permute-start | bytes 589832 | tf_op jit(solution)/shard_map/ppermute | solution.py:588
  400.9 17.5 %collective-permute-start.59 = (bf16[128,512]{1,0:T(8,128)(2,1)S(1)}, bf16[128,512]{1,0:T(8,128)(2,1)S(1)}, u32[]{:S(2)}, u32[]{:S(2)}) collective-permute-start(bf16[128,512]{1,0:T(8,128)(2,1)S(1)} %pad_maximum_fusion.18), channel_id=1, source_target_pairs={{0,1},{1,0},{2,3},{3,2},{4,5},{5,4},{6,7},{7,6},{8,9},{9,8},{10,11... | collective-permute-start | bytes 393224 | tf_op jit(solution)/shard_map/ppermute | solution.py:588
  403.3 15.1 %collective-permute-start.60 = (bf16[128,512]{1,0:T(8,128)(2,1)S(1)}, bf16[128,512]{1,0:T(8,128)(2,1)S(1)}, u32[]{:S(2)}, u32[]{:S(2)}) collective-permute-start(bf16[128,512]{1,0:T(8,128)(2,1)S(1)} %pad_maximum_fusion.19), channel_id=1, source_target_pairs={{0,2},{1,3},{2,0},{3,1},{4,6},{5,7},{6,4},{7,5},{8,10},{9,11},{10,... | collective-permute-start | bytes 393224 | tf_op jit(solution)/shard_map/ppermute | solution.py:588
  (145 other events, 1145.1 us)
Sparse Core Ops, SparseCore 0:
  10.9 159.0 all-gather.2
where the time goes:
time: 435 us; the launch traced here: 431 us
  Pallas kernels  171 us (39%)
  starting transfers between devices  92.1 us (21%)
  waiting for transfers between devices  82.8 us (19%)
  local copies, waits for them, and re-layouts  37.9 us (9%)
  other arithmetic  30.5 us (7%)
  between operations  16.5 us (4%)
    pallas_call x19, Pallas kernels, call(): return lambda *args: run(*args, *hold)  113 us
    pallas_call x4, Pallas kernels, per_device(): pl.pallas_call(kernel, grid_spec=pltpu.PrefetchScalarGridSpec(num_scalar_...  57.7 us
    ppermute x24, starting transfers between devices, swap_tensor(): lax.ppermute(values, 'tensor', [(at, at ^ bit) for at in range(tensor_siz...  56.1 us
    ppermute x39, waiting for transfers between devices, swap_dp(): return lax.ppermute(values, 'dp', [(at, at ^ bit) for at in range(dp_size)])  47.8 us
    ppermute x39, starting transfers between devices, swap_dp(): return lax.ppermute(values, 'dp', [(at, at ^ bit) for at in range(dp_size)])  31.8 us
    unnamed x232, local copies, waits for them, and re-layouts  30.2 us
    ppermute x24, waiting for transfers between devices, swap_tensor(): lax.ppermute(values, 'tensor', [(at, at ^ bit) for at in range(tensor_siz...  29.7 us
    convert_element_type x28, other arithmetic, add(): return (one.astype(f32) + two.astype(f32)).astype(one.dtype)  24.9 us
  transfers between devices with their start and end apart: 66, of which 21 were waited for; matrix products, arithmetic and copies ran while one was open for 8% of the time, Pallas kernels for 36%

commit v1 on v0

--- a/solution.py
+++ b/solution.py
@@ -793,12 +793,12 @@
             tuple(in_near[1:]) + (first_rows, branch_gate, mixer_out)
         )
         in_gathers = [Gather(values, orders[at % 2]) for at, values in enumerate(in_pairs_of(in_near))]
+        gate_weights, out_weights, hidden_low = round_of(in_gathers, gate_weights, out_weights, hidden_low)
         out_near = spread_tensor(jnp.concatenate([gate_weights, out_weights], axis=1))
-        *out_near[1:], hidden_low = round_of(in_gathers, *out_near[1:], hidden_low)
+        out_near[1:] = round_of(in_gathers, *out_near[1:])
         out_gathers = [
             Gather(interleave(one, two), orders[at % 2]) for at, (one, two) in enumerate(zip(out_near[0::2], out_near[1::2]))
         ]
-        round_of(in_gathers + out_gathers)
         in_pairs = [one.finish() for one in in_gathers]
         if not merged:
             small_low, small_high = Gather(jnp.concatenate(spread_tensor(small), axis=1), order_one).finish()
@@ -853,6 +853,8 @@
                 )(normed_one, low, high, rgates[part], igates[part], table[:, lanes])
             )
             fed[pair] = list(fed[pair])
+            if pair == 0:
+                fed[pair][5:] = round_of(out_gathers, fed[pair][5])
         fed[-1][5:] = round_of(out_gathers, fed[-1][5])
         out_pairs = [one.finish() for one in out_gathers]
 

time: 435 us -> 428 us (0.984)
  waiting for transfers between devices: 82.8 us -> 91.4 us
  starting transfers between devices: 92.1 us -> 84.8 us
    ppermute x24, waiting for transfers between devices: 29.7 us -> 45.6 us  [swap_tensor(): lax.ppermute(values, 'tensor', [(at, at ^ bit) for at in range(tensor_siz...]
    ppermute x39, waiting for transfers between devices: 47.8 us -> 39.1 us  [swap_dp(): return lax.ppermute(values, 'dp', [(at, at ^ bit) for at in range(dp_size)])]
    ppermute x24, starting transfers between devices: 56.1 us -> 47.6 us  [swap_tensor(): lax.ppermute(values, 'tensor', [(at, at ^ bit) for at in range(tensor_siz...]
    unnamed x232 -> x206, local copies, waits for them, and re-layouts: 30.2 us -> 31.5 us
  transfers between devices with their start and end apart: 66 -> 66, of which waited for: 21 -> 24; matrix products, arithmetic and copies ran while one was open for 8% -> 6% of each run, Pallas kernels for 36% -> 36%
where the time goes in v1:
time: 428 us; the launch traced here: 424 us
  Pallas kernels  168 us (39%)
  waiting for transfers between devices  91.4 us (21%)
  starting transfers between devices  84.8 us (20%)
  local copies, waits for them, and re-layouts  36.9 us (9%)
  other arithmetic  26.3 us (6%)
  between operations  16.3 us (4%)
    pallas_call x19, Pallas kernels, call(): return lambda *args: run(*args, *hold)  110 us
    pallas_call x4, Pallas kernels, per_device(): pl.pallas_call(kernel, grid_spec=pltpu.PrefetchScalarGridSpec(num_scalar_...  57.7 us
    ppermute x24, starting transfers between devices, swap_tensor(): lax.ppermute(values, 'tensor', [(at, at ^ bit) for at in range(tensor_siz...  47.6 us
    ppermute x24, waiting for transfers between devices, swap_tensor(): lax.ppermute(values, 'tensor', [(at, at ^ bit) for at in range(tensor_siz...  45.6 us
    ppermute x39, waiting for transfers between devices, swap_dp(): return lax.ppermute(values, 'dp', [(at, at ^ bit) for at in range(dp_size)])  39.1 us
    ppermute x39, starting transfers between devices, swap_dp(): return lax.ppermute(values, 'dp', [(at, at ^ bit) for at in range(dp_size)])  33 us
    unnamed x206, local copies, waits for them, and re-layouts  31.5 us
    convert_element_type x28, other arithmetic, add(): return (one.astype(f32) + two.astype(f32)).astype(one.dtype)  21.2 us
  transfers between devices with their start and end apart: 66, of which 24 were waited for; matrix products, arithmetic and copies ran while one was open for 6% of the time, Pallas kernels for 36%

profile of v1, /device:TPU:0, one launch (start us, length us, event | category | flops | bytes accessed | tf_op | source)
XLA Modules:
  0.0 423.7 jit_solution(9475198396271061155)
XLA Ops:
  10.0 3.1 collective-permute-start
  18.5 3.7 collective-permute-done.3.refs_2_
  22.2 3.8 collective-permute-done.1
  37.3 4.1 collective-permute-start.10
  41.4 12.5 %collective-permute-start.8 = (bf16[128,768]{1,0:T(8,128)(2,1)S(1)}, bf16[128,768]{1,0:T(8,128)(2,1)S(1)}, u32[]{:S(2)}, u32[]{:S(2)}) collective-permute-start(bf16[128,768]{1,0:T(8,128)(2,1)S(1)} %constant_dynamic-update-slice_fusion), channel_id=1, source_target_pairs={{0,1},{1,0},{2,3},{3,2},{4,5},{5,4},{6,7},{7,6},{8,9},{9,8},{10,11... | collective-permute-start | bytes 589832 | tf_op jit(solution)/shard_map/ppermute | solution.py:588
  54.0 11.7 %collective-permute-done.8 = bf16[128,768]{1,0:T(8,128)(2,1)S(1)} collective-permute-done((bf16[128,768]{1,0:T(8,128)(2,1)S(1)}, bf16[128,768]{1,0:T(8,128)(2,1)S(1)}, u32[]{:S(2)}, u32[]{:S(2)}) %collective-permute-start.8) | collective-permute-done | bytes 196640 | tf_op jit(solution)/shard_map/ppermute | solution.py:588
  65.7 13.7 %collective-permute-done.9 = bf16[128,768]{1,0:T(8,128)(2,1)S(1)} collective-permute-done((bf16[128,768]{1,0:T(8,128)(2,1)S(1)}, bf16[128,768]{1,0:T(8,128)(2,1)S(1)}, u32[]{:S(2)}, u32[]{:S(2)}) %collective-permute-start.9) | collective-permute-done | bytes 196640 | tf_op jit(solution)/shard_map/ppermute | solution.py:588
  86.0 2.9 norm_kernel.1
  89.1 11.4 %mix_in_kernel.2 = (f32[528,768]{1,0:T(8,128)S(1)}, f32[512,768]{1,0:T(8,128)S(1)}, f32[512,768]{1,0:T(8,128)S(1)}, f32[512,768]{1,0:T(8,128)S(1)}, f32[512,768]{1,0:T(8,128)S(1)}, /*index=5*/f32[512,768]{1,0:T(8,128)S(1)}) custom-call(bf16[528,1024]{1,0:T(8,128)(2,1)S(1)} %get-tuple-element.198.refs_0_, ...), custom_call_target="tpu_custom_call" | custom-call | flops 16099999744 | tf_op jit(solution)/shard_map/mix_in_kernel/pallas_call | solution.py:573
  107.3 11.4 %mix_in_kernel.3 = (f32[528,768]{1,0:T(8,128)S(1)}, f32[512,768]{1,0:T(8,128)S(1)}, f32[512,768]{1,0:T(8,128)S(1)}, f32[512,768]{1,0:T(8,128)S(1)}, f32[512,768]{1,0:T(8,128)S(1)}, /*index=5*/f32[512,768]{1,0:T(8,128)S(1)}) custom-call(bf16[528,1024]{1,0:T(8,128)(2,1)S(1)} %get-tuple-element.198.refs_0_, ...), custom_call_target="tpu_custom_call" | custom-call | flops 16099999744 | tf_op jit(solution)/shard_map/mix_in_kernel/pallas_call | solution.py:573
  121.0 20.1 %collective-permute-done.16 = bf16[256,1536]{1,0:T(8,128)(2,1)S(1)} collective-permute-done((bf16[256,1536]{1,0:T(8,128)(2,1)S(1)}, bf16[256,1536]{1,0:T(8,128)(2,1)S(1)}, u32[]{:S(2)}, u32[]{:S(2)}) %collective-permute-start.16) | collective-permute-done | bytes 786464 | tf_op jit(solution)/shard_map/ppermute | solution.py:585
  144.0 2.9 collective-permute-start.19
  152.5 6.4 %mix_out_kernel.2 = (f32[512,768]{1,0:T(8,128)S(1)}, f32[520,768]{1,0:T(8,128)S(1)}, bf16[512,768]{1,0:T(8,128)(2,1)S(1)}, f32[512,1024]{1,0:T(8,128)S(1)}) custom-call(bf16[528,1024]{1,0:T(8,128)(2,1)S(1)} %get-tuple-element.198.refs_0_, bf16[512,1536]{1,0:T(8,128)(2,1)S(1)} %pad_maximum_fusion.1.refs_1_.refs_3_, ...), custom_call_target="tpu_custom_call" | custom-call | flops 11500000256 | tf_op jit(solution)/shard_map/mix_out_kernel/pallas_call | solution.py:573
  162.2 6.4 %mix_out_kernel.3 = (f32[512,768]{1,0:T(8,128)S(1)}, f32[520,768]{1,0:T(8,128)S(1)}, bf16[512,768]{1,0:T(8,128)(2,1)S(1)}, f32[512,1024]{1,0:T(8,128)S(1)}) custom-call(bf16[528,1024]{1,0:T(8,128)(2,1)S(1)} %get-tuple-element.198.refs_0_, bf16[512,1536]{1,0:T(8,128)(2,1)S(1)} %pad_maximum_fusion.refs_1_.refs_3_, ...), custom_call_target="tpu_custom_call" | custom-call | flops 11500000256 | tf_op jit(solution)/shard_map/mix_out_kernel/pallas_call | solution.py:573
  182.8 14.2 %mlp_kernel.4 = (f32[512,1024]{1,0:T(8,128)S(1)}, f32[512,1024]{1,0:T(8,128)S(1)}, bf16[512,2304]{1,0:T(8,128)(2,1)S(1)}, bf16[512,2304]{1,0:T(8,128)(2,1)S(1)}) custom-call(s32[4]{0:T(128)S(1)} %iota_xor_fusion.refs_0_, bf16[512,1024]{1,0:T(8,128)(2,1)S(1)} %copy-done.29, bf16[1024,512]{1,0:T(8,128)(2,1)S(1)} %copy-done.31, ...), custom_call_target="tpu_custom_call" | custom-call | flops 19549999104 | tf_op jit(solution)/shard_map/mlp_kernel/pallas_call | solution.py:916
  197.1 14.7 %mlp_kernel.5 = (f32[512,1024]{1,0:T(8,128)S(1)}, f32[512,1024]{1,0:T(8,128)S(1)}, bf16[512,2304]{1,0:T(8,128)(2,1)S(1)}, bf16[512,2304]{1,0:T(8,128)(2,1)S(1)}) custom-call(s32[4]{0:T(128)S(1)} %iota_xor_fusion.refs_0_, bf16[512,1024]{1,0:T(8,128)(2,1)S(1)} %copy-done.29, bf16[1024,512]{1,0:T(8,128)(2,1)S(1)} %copy-done.31, ...), custom_call_target="tpu_custom_call" | custom-call | flops 19549999104 | tf_op jit(solution)/shard_map/mlp_kernel/pallas_call | solution.py:916
  214.0 14.2 %mlp_kernel.6 = (f32[512,1024]{1,0:T(8,128)S(1)}, f32[512,1024]{1,0:T(8,128)S(1)}, bf16[512,2304]{1,0:T(8,128)(2,1)S(1)}, bf16[512,2304]{1,0:T(8,128)(2,1)S(1)}) custom-call(s32[4]{0:T(128)S(1)} %iota_xor_fusion.refs_0_, bf16[512,1024]{1,0:T(8,128)(2,1)S(1)} %copy-done.29, bf16[1024,512]{1,0:T(8,128)(2,1)S(1)} %copy-done.31, ...), custom_call_target="tpu_custom_call" | custom-call | flops 19549999104 | tf_op jit(solution)/shard_map/mlp_kernel/pallas_call | solution.py:916
  230.9 14.5 %mlp_kernel.7 = (f32[512,1024]{1,0:T(8,128)S(1)}, f32[512,1024]{1,0:T(8,128)S(1)}, bf16[512,2304]{1,0:T(8,128)(2,1)S(1)}, bf16[512,2304]{1,0:T(8,128)(2,1)S(1)}) custom-call(s32[4]{0:T(128)S(1)} %iota_xor_fusion.refs_0_, bf16[512,1024]{1,0:T(8,128)(2,1)S(1)} %copy-done.29, bf16[1024,512]{1,0:T(8,128)(2,1)S(1)} %copy-done.31, ...), custom_call_target="tpu_custom_call" | custom-call | flops 19549999104 | tf_op jit(solution)/shard_map/mlp_kernel/pallas_call | solution.py:916
  249.1 6.1 %middle_kernel.1 = (bf16[512,1024]{1,0:T(8,128)(2,1)}, f32[512,1024]{1,0:T(8,128)S(1)}, bf16[512,1024]{1,0:T(8,128)(2,1)S(1)}, bf16[1024,512]{1,0:T(8,128)(2,1)S(1)}, f32[1,1024]{1,0:T(1,128)S(1)}) custom-call(s32[8]{0:T(128)S(1)} %broadcast_xor_fusion.refs_0_, f32[512,1024]{1,0:T(8,128)S(1)} %copy-done.38, f32[512,1024]{1,0:T(8,128)S(1)} %get-tuple-element.236.refs_2_, ...), custom_call_target="tpu_custom_call" | custom-call | flops 13799999488 | tf_op jit(solution)/shard_map/middle_kernel/pallas_call | solution.py:573
  258.8 3.5 add_convert_fusion
  263.3 13.7 %mix_back.2 = (f32[512,1024]{1,0:T(8,128)S(1)}, f32[512,768]{1,0:T(8,128)S(1)}, f32[512,768]{1,0:T(8,128)S(1)}, f32[8,768]{1,0:T(8,128)S(1)}, bf16[512,1536]{1,0...) custom-call(bf16[512,1024]{1,0:T(8,128)(2,1)S(1)} %get-tuple-element.242.refs_0_, ...), custom_call_target="tpu_custom_call" | custom-call | flops 20700000256 | tf_op jit(solution)/shard_map/mix_back/pallas_call | solution.py:573
  283.0 13.7 %mix_back.3 = (f32[512,1024]{1,0:T(8,128)S(1)}, f32[512,768]{1,0:T(8,128)S(1)}, f32[512,768]{1,0:T(8,128)S(1)}, f32[8,768]{1,0:T(8,128)S(1)}, bf16[512,1536]{1,0...) custom-call(bf16[512,1024]{1,0:T(8,128)(2,1)S(1)} %get-tuple-element.242.refs_0_, ...), custom_call_target="tpu_custom_call" | custom-call | flops 20700000256 | tf_op jit(solution)/shard_map/mix_back/pallas_call | solution.py:573
  303.2 3.6 collective-permute-done.34
  312.5 8.4 %gate_back_kernel.2 = (f32[512,768]{1,0:T(8,128)S(1)}, f32[6,128,128]{2,1,0:T(8,128)S(1)}, f32[6,128,128]{2,1,0:T(8,128)S(1)}, f32[8,768]{1,0:T(8,128)S(1)}) custom-call(f32[512,768]{1,0:T(8,128)S(1)} %copy-done.73, f32[512,768]{1,0:T(8,128)S(1)} %copy-done.75, f32[1,768]{1,0:T(1,128)S(1)} %get-tuple-element.490.refs_2_, f32[520,768]{1,0:T(8,128)S(1)} %copy-done.47, ...), custom_call_target="tpu_custom_call" | custom-call | flops 12650000384 | tf_op jit(solution)/shard_map/gate_back_kernel/pallas_call | solution.py:573
  327.8 8.6 %gate_back_kernel.3 = (f32[512,768]{1,0:T(8,128)S(1)}, f32[6,128,128]{2,1,0:T(8,128)S(1)}, f32[6,128,128]{2,1,0:T(8,128)S(1)}, f32[8,768]{1,0:T(8,128)S(1)}) custom-call(f32[512,768]{1,0:T(8,128)S(1)} %copy-done.64, f32[512,768]{1,0:T(8,128)S(1)} %get-tuple-element.267.refs_1_, f32[1,768]{1,0:T(1,128)S(1)} %get-tuple-element.491.refs_2_, ...), custom_call_target="tpu_custom_call" | custom-call | flops 12650000384 | tf_op jit(solution)/shard_map/gate_back_kernel/pallas_call | solution.py:573
  341.5 3.0 collective-permute-done.40
  344.6 3.7 collective-permute-start.63
  350.9 4.4 %branch_back.2 = (f32[512,1024]{1,0:T(8,128)S(1)}, bf16[512,1024]{1,0:T(8,128)(2,1)S(1)}, bf16[512,1024]{1,0:T(8,128)(2,1)S(1)}) custom-call(f32[512,768]{1,0:T(8,128)S(1)} %get-tuple-element.297.refs_0_, f32[8,768]{1,0:T(8,128)S(1)} %get-tuple-element.454.refs_1_, f32[8,768]{1,0:T(8,128)S(1)} %get-tuple-element.460.refs_5_.refs_9_.refs_10_.refs_2_, ...), custom_call_target="tpu_custom_call" | custom-call | flops 9200000000 | tf_op jit(solution)/shard_map/branch_back/pallas_call | solution.py:573
  357.7 4.3 %collective-permute-done.41 = bf16[128,1536]{1,0:T(8,128)(2,1)S(1)} collective-permute-done((bf16[128,1536]{1,0:T(8,128)(2,1)S(1)}, bf16[128,1536]{1,0:T(8,128)(2,1)S(1)}, u32[]{:S(2)}, u32[]{:S(2)}) %collective-permute-start.41) | collective-permute-done | bytes 393248 | tf_op jit(solution)/shard_map/ppermute | solution.py:585
  363.4 4.3 %branch_back.3 = (f32[512,1024]{1,0:T(8,128)S(1)}, bf16[512,1024]{1,0:T(8,128)(2,1)S(1)}, bf16[512,1024]{1,0:T(8,128)(2,1)S(1)}) custom-call(f32[512,768]{1,0:T(8,128)S(1)} %get-tuple-element.292.refs_0_, f32[8,768]{1,0:T(8,128)S(1)} %get-tuple-element.455.refs_1_, f32[8,768]{1,0:T(8,128)S(1)} %copy-done.16, bf16[1024,512]{1,0:T(8,128)(2,1)S(1)} %copy-done.43, ...), custom_call_target="tpu_custom_call" | custom-call | flops 9200000000 | tf_op jit(solution)/shard_map/branch_back/pallas_call | solution.py:573
  375.1 5.5 %final_kernel.1 = (f32[512,1024]{1,0:T(8,128)}, f32[1,1024]{1,0:T(1,128)S(1)}) custom-call(s32[8]{0:T(128)S(1)} %broadcast_xor_fusion.refs_0_, bf16[512,1024]{1,0:T(8,128)(2,1)S(1)} %copy-done.34, f32[512,1024]{1,0:T(8,128)S(1)} %get-tuple-element.325.refs_2_, f32[512,1024]{1,0:T(8,128)S(1)} %copy-done.45, ...), custom_call_target="tpu_custom_call" | custom-call | flops 11500000256 | tf_op jit(solution)/shard_map/final_kernel/pallas_call | solution.py:573
  380.8 3.9 collective-permute-done.47
  (475 shorter events, 149.0 us)
Async XLA Ops:
  7.3 170.6 %all-gather.3.cloned.1.call-start = ((), (), s32[]{:S(2)}) async-start(), calls=%async_computation | async-start | bytes 19464192 | tf_op jit(solution)/shard_map/all_gather | solution.py:805
  35.1 44.3 %collective-permute-start.7 = (bf16[256,1024]{1,0:T(8,128)(2,1)S(1)}, bf16[256,1024]{1,0:T(8,128)(2,1)S(1)}, u32[]{:S(2)}, u32[]{:S(2)}) collective-permute-start(bf16[256,1024]{1,0:T(8,128)(2,1)S(1)} %pad_maximum_fusion.10), channel_id=1, source_target_pairs={{0,8},{4,12},{8,0},{12,4},{16,24},{20,28},{24,16},{28,20},{1,9},{5... | collective-permute-start | bytes 1572872 | tf_op jit(solution)/shard_map/ppermute | solution.py:585
  36.7 42.7 %collective-permute-start.6 = (bf16[256,1024]{1,0:T(8,128)(2,1)S(1)}, bf16[256,1024]{1,0:T(8,128)(2,1)S(1)}, u32[]{:S(2)}, u32[]{:S(2)}) collective-permute-start(bf16[256,1024]{1,0:T(8,128)(2,1)S(1)} %pad_maximum_fusion.9), channel_id=1, source_target_pairs={{0,16},{4,20},{8,24},{12,28},{16,0},{20,4},{24,8},{28,12},{1,17},{... | collective-permute-start | bytes 1572872 | tf_op jit(solution)/shard_map/ppermute | solution.py:585
  37.3 16.6 %collective-permute-start.10 = (bf16[128,768]{1,0:T(8,128)(2,1)S(1)}, bf16[128,768]{1,0:T(8,128)(2,1)S(1)}, u32[]{:S(2)}, u32[]{:S(2)}) collective-permute-start(bf16[128,768]{1,0:T(8,128)(2,1)S(1)} %constant_dynamic-update-slice_fusion), channel_id=1, source_target_pairs={{0,3},{1,2},{2,1},{3,0},{4,7},{5,6},{6,5},{7,4},{8,11},{9,10},{10,... | collective-permute-start | bytes 589832 | tf_op jit(solution)/shard_map/ppermute | solution.py:588
  41.4 24.2 %collective-permute-start.8 = (bf16[128,768]{1,0:T(8,128)(2,1)S(1)}, bf16[128,768]{1,0:T(8,128)(2,1)S(1)}, u32[]{:S(2)}, u32[]{:S(2)}) collective-permute-start(bf16[128,768]{1,0:T(8,128)(2,1)S(1)} %constant_dynamic-update-slice_fusion), channel_id=1, source_target_pairs={{0,1},{1,0},{2,3},{3,2},{4,5},{5,4},{6,7},{7,6},{8,9},{9,8},{10,11... | collective-permute-start | bytes 589832 | tf_op jit(solution)/shard_map/ppermute | solution.py:588
  53.9 25.4 %collective-permute-start.9 = (bf16[128,768]{1,0:T(8,128)(2,1)S(1)}, bf16[128,768]{1,0:T(8,128)(2,1)S(1)}, u32[]{:S(2)}, u32[]{:S(2)}) collective-permute-start(bf16[128,768]{1,0:T(8,128)(2,1)S(1)} %constant_dynamic-update-slice_fusion), channel_id=1, source_target_pairs={{0,2},{1,3},{2,0},{3,1},{4,6},{5,7},{6,4},{7,5},{8,10},{9,11},{10,... | collective-permute-start | bytes 589832 | tf_op jit(solution)/shard_map/ppermute | solution.py:588
  80.5 23.6 %collective-permute-start.14 = (bf16[128,1536]{1,0:T(8,128)(2,1)S(1)}, bf16[128,1536]{1,0:T(8,128)(2,1)S(1)}, u32[]{:S(2)}, u32[]{:S(2)}) collective-permute-start(bf16[128,1536]{1,0:T(8,128)(2,1)S(1)} %slice_dynamic-update-slice_fusion.4), channel_id=1, source_target_pairs={{0,16},{4,20},{8,24},{12,28},{16,0},{20,4},{24,8},{28,12},{1,17},{... | collective-permute-start | bytes 1179656 | tf_op jit(solution)/shard_map/ppermute | solution.py:585
  82.3 21.7 %collective-permute-start.13 = (bf16[128,1536]{1,0:T(8,128)(2,1)S(1)}, bf16[128,1536]{1,0:T(8,128)(2,1)S(1)}, u32[]{:S(2)}, u32[]{:S(2)}) collective-permute-start(bf16[128,1536]{1,0:T(8,128)(2,1)S(1)} %slice_dynamic-update-slice_fusion), channel_id=1, source_target_pairs={{0,8},{4,12},{8,0},{12,4},{16,24},{20,28},{24,16},{28,20},{1,9},{5... | collective-permute-start | bytes 1179656 | tf_op jit(solution)/shard_map/ppermute | solution.py:585
  104.1 37.1 %collective-permute-start.16 = (bf16[256,1536]{1,0:T(8,128)(2,1)S(1)}, bf16[256,1536]{1,0:T(8,128)(2,1)S(1)}, u32[]{:S(2)}, u32[]{:S(2)}) collective-permute-start(bf16[256,1536]{1,0:T(8,128)(2,1)S(1)} %pad_maximum_fusion.5), channel_id=1, source_target_pairs={{0,8},{4,12},{8,0},{12,4},{16,24},{20,28},{24,16},{28,20},{1,9},{5... | collective-permute-start | bytes 2359304 | tf_op jit(solution)/shard_map/ppermute | solution.py:585
  106.0 37.0 %collective-permute-start.15 = (bf16[256,1536]{1,0:T(8,128)(2,1)S(1)}, bf16[256,1536]{1,0:T(8,128)(2,1)S(1)}, u32[]{:S(2)}, u32[]{:S(2)}) collective-permute-start(bf16[256,1536]{1,0:T(8,128)(2,1)S(1)} %pad_maximum_fusion.4), channel_id=1, source_target_pairs={{0,16},{4,20},{8,24},{12,28},{16,0},{20,4},{24,8},{28,12},{1,17},{... | collective-permute-start | bytes 2359304 | tf_op jit(solution)/shard_map/ppermute | solution.py:585
  197.0 15.5 %collective-permute-start.22 = (bf16[512,2304]{1,0:T(8,128)(2,1)S(1)}, bf16[512,2304]{1,0:T(8,128)(2,1)S(1)}, u32[]{:S(2)}, u32[]{:S(2)}) collective-permute-start(bf16[512,2304]{1,0:T(8,128)(2,1)S(1)} %get-tuple-element.220), channel_id=1, source_target_pairs={{0,4},{4,0},{8,12},{12,8},{16,20},{20,16},{24,28},{28,24},{1,5},{5... | collective-permute-start | bytes 7077896 | tf_op jit(solution)/shard_map/ppermute | solution.py:585
  211.8 16.4 %collective-permute-start.24 = (bf16[512,2304]{1,0:T(8,128)(2,1)S(1)}, bf16[512,2304]{1,0:T(8,128)(2,1)S(1)}, u32[]{:S(2)}, u32[]{:S(2)}) collective-permute-start(bf16[512,2304]{1,0:T(8,128)(2,1)S(1)} %get-tuple-element.229), channel_id=1, source_target_pairs={{0,4},{4,0},{8,12},{12,8},{16,20},{20,16},{24,28},{28,24},{1,5},{5... | collective-permute-start | bytes 7077896 | tf_op jit(solution)/shard_map/ppermute | solution.py:585
  213.0 43.4 %collective-permute-start.25 = (bf16[256,2304]{1,0:T(8,128)(2,1)S(1)}, bf16[256,2304]{1,0:T(8,128)(2,1)}, u32[]{:S(2)}, u32[]{:S(2)}) collective-permute-start(bf16[256,2304]{1,0:T(8,128)(2,1)S(1)} %add_convert_fusion.7.refs_10_), channel_id=1, source_target_pairs={{0,8},{4,12},{8,0},{12,4},{16,24},{20,28},{24,16},{28,20},{1,9},{5... | collective-permute-start | bytes 3538952 | tf_op jit(solution)/shard_map/ppermute | solution.py:585
  228.2 17.9 %collective-permute-start.23 = (bf16[512,2304]{1,0:T(8,128)(2,1)S(1)}, bf16[512,2304]{1,0:T(8,128)(2,1)S(1)}, u32[]{:S(2)}, u32[]{:S(2)}) collective-permute-start(bf16[512,2304]{1,0:T(8,128)(2,1)S(1)} %get-tuple-element.228), channel_id=1, source_target_pairs={{0,4},{4,0},{8,12},{12,8},{16,20},{20,16},{24,28},{28,24},{1,5},{5... | collective-permute-start | bytes 7077896 | tf_op jit(solution)/shard_map/ppermute | solution.py:585
  230.0 47.0 %collective-permute-start.28 = (bf16[256,2304]{1,0:T(8,128)(2,1)S(1)}, bf16[256,2304]{1,0:T(8,128)(2,1)}, u32[]{:S(2)}, u32[]{:S(2)}) collective-permute-start(bf16[256,2304]{1,0:T(8,128)(2,1)S(1)} %get-tuple-element.369.refs_10_), channel_id=1, source_target_pairs={{0,16},{4,20},{8,24},{12,28},{16,0},{20,4},{24,8},{28,12},{1,17},{... | collective-permute-start | bytes 3538952 | tf_op jit(solution)/shard_map/ppermute | solution.py:585
  247.4 59.5 %collective-permute-start.30 = (bf16[256,2304]{1,0:T(8,128)(2,1)S(1)}, bf16[256,2304]{1,0:T(8,128)(2,1)}, u32[]{:S(2)}, u32[]{:S(2)}) collective-permute-start(bf16[256,2304]{1,0:T(8,128)(2,1)S(1)} %add_convert_fusion.5.refs_6_), channel_id=1, source_target_pairs={{0,8},{4,12},{8,0},{12,4},{16,24},{20,28},{24,16},{28,20},{1,9},{5... | collective-permute-start | bytes 3538952 | tf_op jit(solution)/shard_map/ppermute | solution.py:585
  257.7 22.8 %collective-permute-start.27 = (bf16[128,2304]{1,0:T(8,128)(2,1)S(1)}, bf16[128,2304]{1,0:T(8,128)(2,1)S(1)}, u32[]{:S(2)}, u32[]{:S(2)}) collective-permute-start(bf16[128,2304]{1,0:T(8,128)(2,1)S(1)} %add_convert_fusion.23.refs_12_), channel_id=1, source_target_pairs={{0,16},{4,20},{8,24},{12,28},{16,0},{20,4},{24,8},{28,12},{1,17},{... | collective-permute-start | bytes 1769480 | tf_op jit(solution)/shard_map/ppermute | solution.py:585
  262.2 58.6 %collective-permute-start.36 = (bf16[256,2304]{1,0:T(8,128)(2,1)S(1)}, bf16[256,2304]{1,0:T(8,128)(2,1)}, u32[]{:S(2)}, u32[]{:S(2)}) collective-permute-start(bf16[256,2304]{1,0:T(8,128)(2,1)S(1)} %get-tuple-element.367.refs_11_), channel_id=1, source_target_pairs={{0,16},{4,20},{8,24},{12,28},{16,0},{20,4},{24,8},{28,12},{1,17},{... | collective-permute-start | bytes 3538952 | tf_op jit(solution)/shard_map/ppermute | solution.py:585
  278.8 17.9 %collective-permute-start.31 = (bf16[128,2304]{1,0:T(8,128)(2,1)S(1)}, bf16[128,2304]{1,0:T(8,128)(2,1)S(1)}, u32[]{:S(2)}, u32[]{:S(2)}) collective-permute-start(bf16[128,2304]{1,0:T(8,128)(2,1)S(1)} %add_convert_fusion.22.refs_12_), channel_id=1, source_target_pairs={{0,8},{4,12},{8,0},{12,4},{16,24},{20,28},{24,16},{28,20},{1,9},{5... | collective-permute-start | bytes 1769480 | tf_op jit(solution)/shard_map/ppermute | solution.py:585
  280.1 28.9 %collective-permute-start.29 = (bf16[512,1536]{1,0:T(8,128)(2,1)S(1)}, bf16[512,1536]{1,0:T(8,128)(2,1)}, u32[]{:S(2)}, u32[]{:S(2)}) collective-permute-start(bf16[512,1536]{1,0:T(8,128)(2,1)S(1)} %get-tuple-element.268), channel_id=1, source_target_pairs={{0,4},{4,0},{8,12},{12,8},{16,20},{20,16},{24,28},{28,24},{1,5},{5... | collective-permute-start | bytes 4718600 | tf_op jit(solution)/shard_map/ppermute | solution.py:585
  303.1 22.1 %collective-permute-start.35 = (bf16[512,1536]{1,0:T(8,128)(2,1)S(1)}, bf16[512,1536]{1,0:T(8,128)(2,1)S(1)}, u32[]{:S(2)}, u32[]{:S(2)}) collective-permute-start(bf16[512,1536]{1,0:T(8,128)(2,1)S(1)} %get-tuple-element.277), channel_id=1, source_target_pairs={{0,4},{4,0},{8,12},{12,8},{16,20},{20,16},{24,28},{28,24},{1,5},{5... | collective-permute-start | bytes 4718600 | tf_op jit(solution)/shard_map/ppermute | solution.py:585
  308.3 28.0 %collective-permute-start.38 = (bf16[128,2304]{1,0:T(8,128)(2,1)S(1)}, bf16[128,2304]{1,0:T(8,128)(2,1)S(1)}, u32[]{:S(2)}, u32[]{:S(2)}) collective-permute-start(bf16[128,2304]{1,0:T(8,128)(2,1)S(1)} %add_convert_fusion.19.refs_11_), channel_id=1, source_target_pairs={{0,16},{4,20},{8,24},{12,28},{16,0},{20,4},{24,8},{28,12},{1,17},{... | collective-permute-start | bytes 1769480 | tf_op jit(solution)/shard_map/ppermute | solution.py:585
  311.0 37.3 %collective-permute-start.37 = (bf16[256,1536]{1,0:T(8,128)(2,1)S(1)}, bf16[256,1536]{1,0:T(8,128)(2,1)S(1)}, u32[]{:S(2)}, u32[]{:S(2)}) collective-permute-start(bf16[256,1536]{1,0:T(8,128)(2,1)S(1)} %get-tuple-element.371.refs_12_), channel_id=1, source_target_pairs={{0,16},{4,20},{8,24},{12,28},{16,0},{20,4},{24,8},{28,12},{1,17},{... | collective-permute-start | bytes 2359304 | tf_op jit(solution)/shard_map/ppermute | solution.py:585
  320.9 23.7 %collective-permute-start.39 = (bf16[128,2304]{1,0:T(8,128)(2,1)S(1)}, bf16[128,2304]{1,0:T(8,128)(2,1)S(1)}, u32[]{:S(2)}, u32[]{:S(2)}) collective-permute-start(bf16[128,2304]{1,0:T(8,128)(2,1)S(1)} %add_convert_fusion.20.refs_13_), channel_id=1, source_target_pairs={{0,3},{1,2},{2,1},{3,0},{4,7},{5,6},{6,5},{7,4},{8,11},{9,10},{10,... | collective-permute-start | bytes 1769480 | tf_op jit(solution)/shard_map/ppermute | solution.py:588
  324.4 30.9 %collective-permute-start.43 = (bf16[128,2304]{1,0:T(8,128)(2,1)S(1)}, bf16[128,2304]{1,0:T(8,128)(2,1)S(1)}, u32[]{:S(2)}, u32[]{:S(2)}) collective-permute-start(bf16[128,2304]{1,0:T(8,128)(2,1)S(1)} %add_convert_fusion.18.refs_12_), channel_id=1, source_target_pairs={{0,8},{4,12},{8,0},{12,4},{16,24},{20,28},{24,16},{28,20},{1,9},{5... | collective-permute-start | bytes 1769480 | tf_op jit(solution)/shard_map/ppermute | solution.py:585
  337.2 20.5 %collective-permute-start.42 = (bf16[256,1536]{1,0:T(8,128)(2,1)S(1)}, bf16[256,1536]{1,0:T(8,128)(2,1)S(1)}, u32[]{:S(2)}, u32[]{:S(2)}) collective-permute-start(bf16[256,1536]{1,0:T(8,128)(2,1)S(1)} %add_convert_fusion.10.refs_13_), channel_id=1, source_target_pairs={{0,8},{4,12},{8,0},{12,4},{16,24},{20,28},{24,16},{28,20},{1,9},{5... | collective-permute-start | bytes 2359304 | tf_op jit(solution)/shard_map/ppermute | solution.py:585
  344.6 42.5 %collective-permute-start.63 = (bf16[128,2304]{1,0:T(8,128)(2,1)S(1)}, bf16[128,2304]{1,0:T(8,128)(2,1)S(1)}, u32[]{:S(2)}, u32[]{:S(2)}) collective-permute-start(bf16[128,2304]{1,0:T(8,128)(2,1)S(1)} %add_convert_fusion.16.refs_4_.refs_9_), channel_id=1, source_target_pairs={{0,1},{1,0},{2,3},{3,2},{4,5},{5,4},{6,7},{7,6},{8,9},{9,8},{10,11... | collective-permute-start | bytes 1769480 | tf_op jit(solution)/shard_map/ppermute | solution.py:588
  348.3 39.8 %collective-permute-start.64 = (bf16[128,2304]{1,0:T(8,128)(2,1)S(1)}, bf16[128,2304]{1,0:T(8,128)(2,1)S(1)}, u32[]{:S(2)}, u32[]{:S(2)}) collective-permute-start(bf16[128,2304]{1,0:T(8,128)(2,1)S(1)} %add_convert_fusion.14), channel_id=1, source_target_pairs={{0,2},{1,3},{2,0},{3,1},{4,6},{5,7},{6,4},{7,5},{8,10},{9,11},{10,... | collective-permute-start | bytes 1769480 | tf_op jit(solution)/shard_map/ppermute | solution.py:588
  355.3 17.0 %collective-permute-start.45 = (bf16[512,1024]{1,0:T(8,128)(2,1)S(1)}, bf16[512,1024]{1,0:T(8,128)(2,1)S(1)}, u32[]{:S(2)}, u32[]{:S(2)}) collective-permute-start(bf16[512,1024]{1,0:T(8,128)(2,1)S(1)} %get-tuple-element.321), channel_id=1, source_target_pairs={{0,4},{4,0},{8,12},{12,8},{16,20},{20,16},{24,28},{28,24},{1,5},{5... | collective-permute-start | bytes 3145736 | tf_op jit(solution)/shard_map/ppermute | solution.py:585
  370.1 19.1 %collective-permute-start.52 = (bf16[128,768]{1,0:T(8,128)(2,1)S(1)}, bf16[128,768]{1,0:T(8,128)(2,1)S(1)}, u32[]{:S(2)}, u32[]{:S(2)}) collective-permute-start(bf16[128,768]{1,0:T(8,128)(2,1)S(1)} %get-tuple-element.447), channel_id=1, source_target_pairs={{0,3},{1,2},{2,1},{3,0},{4,7},{5,6},{6,5},{7,4},{8,11},{9,10},{10,... | collective-permute-start | bytes 589832 | tf_op jit(solution)/shard_map/ppermute | solution.py:588
  393.9 17.4 %collective-permute-start.59 = (bf16[128,512]{1,0:T(8,128)(2,1)S(1)}, bf16[128,512]{1,0:T(8,128)(2,1)S(1)}, u32[]{:S(2)}, u32[]{:S(2)}) collective-permute-start(bf16[128,512]{1,0:T(8,128)(2,1)S(1)} %pad_maximum_fusion.18), channel_id=1, source_target_pairs={{0,1},{1,0},{2,3},{3,2},{4,5},{5,4},{6,7},{7,6},{8,9},{9,8},{10,11... | collective-permute-start | bytes 393224 | tf_op jit(solution)/shard_map/ppermute | solution.py:588
  396.3 14.9 %collective-permute-start.60 = (bf16[128,512]{1,0:T(8,128)(2,1)S(1)}, bf16[128,512]{1,0:T(8,128)(2,1)S(1)}, u32[]{:S(2)}, u32[]{:S(2)}) collective-permute-start(bf16[128,512]{1,0:T(8,128)(2,1)S(1)} %pad_maximum_fusion.19), channel_id=1, source_target_pairs={{0,2},{1,3},{2,0},{3,1},{4,6},{5,7},{6,4},{7,5},{8,10},{9,11},{10,... | collective-permute-start | bytes 393224 | tf_op jit(solution)/shard_map/ppermute | solution.py:588
  (132 other events, 791.8 us)
Sparse Core Ops, SparseCore 0:
  10.9 157.0 all-gather.2
